TPU v7x, 32 devices: a whole 2x2x4 slice. The times are simulated.
32 devices in a mesh: groups: 2 (over y), ctx: 4 (over z), head: 4 (over x, core).
Axes of the slice: x: 2, y: 2, z: 4, core: 2. Of those that a mesh axis runs over, the one named last changes fastest.
Arguments:
- queries: bfloat16 [4096, 4096], P(('groups', 'ctx', 'head')), parts along dimension 0, may hold values from -6 to 6
- keys_in: bfloat16 [4096, 4096], P(('groups', 'ctx', 'head')), parts along dimension 0, may hold values from -6 to 6
- values: bfloat16 [4096, 4096], P(('groups', 'ctx', 'head')), parts along dimension 0, may hold values from -6 to 6
- doc_lengths: int32 [10], P('groups'), parts along dimension 0, may hold values from 1 to 512, 2048 in all
- rms_gain: float32 [4096], replicated, may hold values from 0.1 to 1.9
Outputs:
- mixed: bfloat16 [4096, 4096], P(('groups', 'ctx', 'head')), parts along dimension 0
There are 2 independent parts, one for each index of `groups`. A program takes and returns all parts, laid end to end along the dimension named above; an argument that names none is the same for every part. Nothing has to cross between parts.
Inputs may be any that keep to these rules, and one draw needn't show every extreme that they name: `doc_lengths`: the lengths of the 5 documents sum to 2048, and the longest has exactly 512 tokens.
All inputs are finite; a program needn't handle non-finite values.
Results may differ from a plain program's by a relative error of at most 0.006.
Values may be sent and summed in bfloat16 or wider, within the bound.
A program may use at most 64 MiB of HBM per device.

v0:
```python
import functools

import jax
import jax.numpy as jnp
from jax import lax
from jax.experimental import pallas as pl
from jax.experimental.pallas import tpu as pltpu
from jax.sharding import PartitionSpec as P

DH = 128
MESH = pl.DeviceIdType.MESH
LIMIT1 = 52 << 20
LIMIT2 = 8 << 20
F32 = jnp.float32
BF16 = jnp.bfloat16


def kv_group(own):
    return 4 if own % 4 == 0 else 1


def silu(v):
    v = v.astype(F32)
    half = 0.5 * v
    return (half + half * jnp.tanh(half)).astype(BF16)


def kernel(nz, nh, docs_hbm, q_hbm, k_hbm, v_hbm, out_ref, scale_ref,
           ends_ref, doc_sem, qb, kb, vb, qa, ka, loc, mask, joinb, keepb, tail, prefix, partial, tin, pin, zin, zout, aout, ain,
           load_sem, ex_send, ex_recv, t_send, t_recv, p_send, p_recv, z_send, z_recv, a_send, a_recv):
    nx = nh // 2
    rows, width = q_hbm.shape
    half = width // 2
    heads = half // DH
    own = heads // nx
    ph = tail.shape[2]
    pieces = own // ph
    docs = ends_ref.shape[0]
    chunk = 2 * rows
    z = lax.axis_index("ctx")
    h = lax.axis_index("head")
    x = h // 2
    c = h % 2
    o = 1 - c

    def device(xx, cc, zz=None):
        return {"ctx": z if zz is None else zz, "head": 2 * xx + cc}

    ahead = [lax.rem(x + 1 + s, nx) for s in range(nx)]
    behind = [lax.rem(x + nx - 1 - s + nx, nx) for s in range(nx)]

    barrier = pltpu.get_barrier_semaphore()
    pl.semaphore_signal(barrier, inc=1, device_id=device(x, o), device_id_type=MESH)
    for s in range(nx - 1):
        pl.semaphore_signal(barrier, inc=1, device_id=device(ahead[s], c), device_id_type=MESH)

    @pl.when(z > 0)
    def _():
        pl.semaphore_signal(barrier, inc=1, device_id=device(x, c, z - 1), device_id_type=MESH)

    @pl.when(z < nz - 1)
    def _():
        pl.semaphore_signal(barrier, inc=1, device_id=device(x, c, z + 1), device_id_type=MESH)

    docs_copy = pltpu.make_async_copy(docs_hbm, ends_ref, doc_sem)
    docs_copy.start()

    ex = ((k_hbm, kb), (v_hbm, vb), (q_hbm, qb))
    eg = kv_group(own)
    small, large = eg * DH, own * DH
    parts = [(s, j, a) for s in range(nx) for j in range(own // eg) for a in (0, 1)]
    parts += [(s, 0, 2) for s in range(nx)]

    def place(s, j, a):
        size = large if a == 2 else small
        return pl.multiple_of(ahead[s] * large + j * small, small), size

    local_copies = {}

    def start_local(keys):
        for s, j, a in keys:
            at, size = place(s, j, a)
            src, dst = ex[a]
            cp = pltpu.make_async_copy(
                src.at[:, pl.ds(pl.multiple_of(c * half + at, small), size)],
                dst.at[c, :, pl.ds(at, size)], load_sem.at[s, j, a])
            cp.start()
            local_copies[s, j, a] = cp

    start_local([k for k in parts if k[2] != 2])

    pl.semaphore_wait(barrier, nx + jnp.where(z > 0, 1, 0) + jnp.where(z < nz - 1, 1, 0))

    ex_copies = {}

    def start_exchange(keys):
        for s, j, a in keys:
            at, size = place(s, j, a)
            src, dst = ex[a]
            cp = pltpu.make_async_remote_copy(
                src_ref=src.at[:, pl.ds(pl.multiple_of(o * half + at, small), size)],
                dst_ref=dst.at[c, :, pl.ds(at, size)],
                send_sem=ex_send.at[s, j, a], recv_sem=ex_recv.at[s, j, a],
                device_id=device(x, o), device_id_type=MESH)
            cp.start()
            ex_copies[s, j, a] = cp

    start_exchange([k for k in parts if k[2] != 2])

    docs_copy.wait()
    ends = [ends_ref[0]]
    for d in range(1, docs):
        ends.append(ends[-1] + ends_ref[d])

    def seg_of(pos):
        total = jnp.where(pos < 0, -1, 0)
        for end in ends:
            total = total + jnp.where(pos >= end, 1, 0)
        return total

    shard_start = z * (nx * chunk)
    first = shard_start + x * chunk
    row_i = lax.broadcasted_iota(jnp.int32, (chunk, DH), 0)
    seg_r = seg_of(row_i + first)
    col_i = lax.broadcasted_iota(jnp.int32, (8, chunk), 1)
    seg_c = seg_of(col_i + first)
    before = seg_of(first - 1)
    last = seg_of(first + chunk - 1)
    joinb[...] = jnp.where(seg_r == before, 1.0, 0.0)
    keepb[...] = jnp.where(seg_r == last, 1.0, 0.0)
    for g in range(chunk // DH):
        sc = jnp.broadcast_to(seg_c[0:1, g * DH:(g + 1) * DH], (chunk, DH))
        ci = lax.broadcasted_iota(jnp.int32, (chunk, DH), 1) + g * DH
        mask[:, g * DH:(g + 1) * DH] = jnp.where((seg_r == sc) & (row_i >= ci), 1.0, 0.0)
    cont = []
    for xx in range(nx):
        f = shard_start + xx * chunk
        cont.append(jnp.where(seg_of(f - 1) == seg_of(f + chunk - 1), 1.0, 0.0).astype(F32))

    def cols(head):
        return pl.ds(pl.multiple_of(head * DH, DH), DH)

    def take(ref, head):
        return ref[:, :, cols(head)].reshape(chunk, DH)

    t_copies = {}
    for s in range(nx):
        for p in range(pieces):
            for i in range(ph):
                if (p * ph + i) % eg == 0:
                    for a in (0, 1):
                        local_copies[s, (p * ph + i) // eg, a].wait()
                        ex_copies[s, (p * ph + i) // eg, a].wait_recv()
                    if s == 0 and p * ph + i == own - eg:
                        start_local([k for k in parts if k[2] == 2])
                        start_exchange([k for k in parts if k[2] == 2])
                head = ahead[s] * own + p * ph + i
                kk = silu(take(kb, head))
                ka[:, cols(head)] = kk
                masked = (kk.astype(F32) * keepb[...]).astype(BF16)
                t = lax.dot_general(masked, take(vb, head), (((0,), (0,)), ((), ())),
                                    preferred_element_type=F32)
                (tin if s == nx - 1 else tail)[s, p, i] = t.astype(BF16)
            if s < nx - 1:
                cp = pltpu.make_async_remote_copy(
                    src_ref=tail.at[s, p], dst_ref=tin.at[s, p],
                    send_sem=t_send.at[s, p], recv_sem=t_recv.at[s, p],
                    device_id=device(ahead[s], c), device_id_type=MESH)
                cp.start()
                t_copies[s, p] = cp

    for s in range(nx):
        local_copies[s, 0, 2].wait()
        ex_copies[s, 0, 2].wait_recv()

    unroll = 2

    def local_heads(step, carry):
        for i in range(unroll):
            head = step * unroll + i
            qq = silu(take(qb, head))
            qa[:, cols(head)] = qq
            scores = lax.dot_general(qq, ka[:, cols(head)], (((1,), (1,)), ((), ())),
                                     preferred_element_type=F32)
            w = (scores * mask[...]).astype(BF16)
            loc[:, cols(head)] = jnp.dot(w, take(vb, head), preferred_element_type=F32)
        return carry

    steps = heads // unroll
    pre = jnp.minimum(z * 4, steps)
    lax.fori_loop(0, pre, local_heads, 0)

    @pl.when(z == 0)
    def _():
        zin[...] = jnp.zeros_like(zin)

    def z_copy(p):
        return pltpu.make_async_remote_copy(
            src_ref=zout.at[p], dst_ref=zin.at[p], send_sem=z_send.at[p], recv_sem=z_recv.at[p],
            device_id=device(x, c, z + 1), device_id_type=MESH)

    p_copies = {}
    for p in range(pieces):
        for s in range(nx - 1):
            t_copies[s, p].wait_recv()
        add, whole = None, 1.0
        for xx in range(nx):
            got = tin[lax.rem(x + 2 * nx - 1 - xx, nx), p].astype(F32)
            add = got if xx == 0 else got + add * cont[xx]
            whole = whole * cont[xx]
            if xx < nx - 1:
                partial[xx] = add
        partial[nx - 1] = add

        @pl.when(z > 0)
        def _():
            z_copy(p).wait_recv()

        carried = zin[p].astype(F32)
        run = partial[nx - 1] + carried * whole
        zout[p] = run.astype(BF16)

        @pl.when(z < nz - 1)
        def _():
            z_copy(p).start()

        passed = 1.0
        prefix[0, p] = zin[p]
        for xx in range(nx - 1):
            passed = passed * cont[xx]
            prefix[xx + 1, p] = (partial[xx] + carried * passed).astype(BF16)
        for s in range(nx - 1):
            cp = pltpu.make_async_remote_copy(
                src_ref=prefix.at[ahead[s], p], dst_ref=pin.at[s, p],
                send_sem=p_send.at[s, p], recv_sem=p_recv.at[s, p],
                device_id=device(ahead[s], c), device_id_type=MESH)
            cp.start()
            p_copies[s, p] = cp
        lax.fori_loop(pre + (steps - pre) * p // pieces, pre + (steps - pre) * (p + 1) // pieces, local_heads, 0)

    a_copies = []
    total = jnp.zeros((rows, DH), F32)

    def finish(head, state):
        inter = jnp.dot(qa[:, cols(head)], state, preferred_element_type=F32)
        att = (loc[:, cols(head)] + inter * joinb[...]).astype(BF16)
        aout[:, :, cols(head)] = att.reshape(2, rows, DH)

    def gather(total, ref, head, side):
        for i in range(ph):
            v = ref[:, cols(head + i)]
            out_ref[:, pl.ds(pl.multiple_of(side * half + (head + i) * DH, DH), DH)] = v
            v = v.astype(F32)
            total = total + v * v
        return total

    late = min(8, heads // ph)
    for s in [nx - 1] + list(range(nx - 1)):
        owner = x if s == nx - 1 else behind[s]
        for p in range(pieces):
            if s < nx - 1:
                p_copies[s, p].wait_recv()
            for i in range(ph):
                state = prefix[x, p, i] if s == nx - 1 else pin[s, p, i]
                finish(owner * own + p * ph + i, state)
            at = pl.ds(pl.multiple_of((owner * own + p * ph) * DH, ph * DH), ph * DH)
            cp = pltpu.make_async_remote_copy(
                src_ref=aout.at[o, :, at], dst_ref=ain.at[:, at],
                send_sem=a_send.at[s, p], recv_sem=a_recv.at[s, p],
                device_id=device(x, o), device_id_type=MESH)
            cp.start()
            a_copies.append((cp, owner * own + p * ph))
            total = gather(total, aout.at[c], owner * own + p * ph, c)
            if len(a_copies) > late:
                done, head = a_copies[-1 - late]
                done.wait_recv()
                total = gather(total, ain, head, o)

    for done, head in a_copies[-late:]:
        done.wait_recv()
        total = gather(total, ain, head, o)
    scale = lax.rsqrt(jnp.sum(total, axis=1, keepdims=True) / width + 1e-05)
    scale_ref[...] = jnp.broadcast_to(scale, (rows, DH))

    for cp in ex_copies.values():
        cp.wait_send()
    for cp in t_copies.values():
        cp.wait_send()
    for cp in p_copies.values():
        cp.wait_send()
    for cp, _ in a_copies:
        cp.wait_send()

    @pl.when(z < nz - 1)
    def _():
        for p in range(pieces):
            z_copy(p).wait_send()


def scale_kernel(parts, att_ref, scale_ref, gain_ref, out_hbm, buf, sems):
    rows, width = att_ref.shape
    part = width // parts
    scale = scale_ref[...]
    copies = []
    for j in range(parts):
        for i in range(part // DH):
            at = j * part + i * DH
            v = att_ref[:, at:at + DH].astype(F32)
            buf[j, :, i * DH:(i + 1) * DH] = (v * scale * gain_ref[0:1, at:at + DH]).astype(BF16)
        cp = pltpu.make_async_copy(buf.at[j], out_hbm.at[:, j * part:(j + 1) * part], sems.at[j])
        cp.start()
        copies.append(cp)
    for cp in copies:
        cp.wait()


def per_device(nz, nh, queries, keys_in, values, doc_lengths, rms_gain):
    rows, width = queries.shape
    nx = nh // 2
    half = width // 2
    heads = half // DH
    own = heads // nx
    ph = 1
    pieces = own // ph
    far = max(nx - 1, 1)
    docs = doc_lengths.shape
    kv = (nx, own // kv_group(own), 3)
    chunk = 2 * rows
    wide = pltpu.VMEM((2, rows, half), BF16)
    flat = pltpu.VMEM((chunk, half), BF16)
    dma = pltpu.SemaphoreType.DMA
    hbm_spec = pl.BlockSpec(memory_space=pltpu.HBM)
    vmem_spec = pl.BlockSpec(memory_space=pltpu.VMEM)
    attended, scale = pl.pallas_call(
        functools.partial(kernel, nz, nh),
        out_shape=(jax.ShapeDtypeStruct((rows, width), BF16), jax.ShapeDtypeStruct((rows, DH), F32)),
        in_specs=[hbm_spec] * 4,
        out_specs=(vmem_spec, vmem_spec),
        scratch_shapes=[
            pltpu.SMEM(docs, jnp.int32), dma(()),
            wide, wide, wide, flat, flat,
            pltpu.VMEM((chunk, half), F32),
            pltpu.VMEM((chunk, chunk), F32),
            pltpu.VMEM((chunk, DH), F32),
            pltpu.VMEM((chunk, DH), F32),
            pltpu.VMEM((far, pieces, ph, DH, DH), BF16),
            pltpu.VMEM((nx, pieces, ph, DH, DH), BF16),
            pltpu.VMEM((nx, ph, DH, DH), F32),
            pltpu.VMEM((nx, pieces, ph, DH, DH), BF16),
            pltpu.VMEM((far, pieces, ph, DH, DH), BF16),
            pltpu.VMEM((pieces, ph, DH, DH), BF16),
            pltpu.VMEM((pieces, ph, DH, DH), BF16),
            wide,
            pltpu.VMEM((rows, half), BF16),
            dma(kv), dma(kv), dma(kv),
            dma((far, pieces)), dma((far, pieces)),
            dma((far, pieces)), dma((far, pieces)),
            dma((pieces,)), dma((pieces,)),
            dma((nx, pieces)), dma((nx, pieces)),
        ],
        compiler_params=pltpu.CompilerParams(collective_id=0, has_side_effects=True, vmem_limit_bytes=LIMIT1),
        name="scan_attention",
    )(pltpu.with_memory_space_constraint(doc_lengths, pltpu.HBM), queries, keys_in, values)
    parts = 4
    return pl.pallas_call(
        functools.partial(scale_kernel, parts),
        out_shape=jax.ShapeDtypeStruct((rows, width), BF16),
        in_specs=[pl.BlockSpec(memory_space=pltpu.VMEM)] * 3,
        out_specs=pl.BlockSpec(memory_space=pl.ANY),
        scratch_shapes=[pltpu.VMEM((parts, rows, width // parts), BF16), dma((parts,))],
        compiler_params=pltpu.CompilerParams(vmem_limit_bytes=LIMIT2),
        name="scale_rows",
    )(attended, scale, rms_gain.reshape(1, width))


def solution(mesh):
    split = P(("groups", "ctx", "head"), None)
    return jax.shard_map(
        functools.partial(per_device, mesh.shape["ctx"], mesh.shape["head"]),
        mesh=mesh,
        in_specs=(split, split, split, P("groups"), P()),
        out_specs=split,
        check_vma=False,
    )
```

profile of v0, /device:TPU:29, one launch (start us, length us, event | category | flops | bytes accessed | tf_op | source)
XLA Modules:
  0.0 25.2 jit_solution(1012577961130762410)
XLA Ops:
  0.0 0.0 copy-start
  0.0 24.1 %scan_attention.1 = (bf16[128,4096]{1,0:T(8,128)(2,1)S(1)}, f32[128,128]{1,0:T(8,128)S(1)}) custom-call(s32[5]{0:T(128)} %docs_hbm.1, bf16[128,4096]{1,0:T(8,128)(2,1)} %q_hbm.1, bf16[128,4096]{1,0:T(8,128)(2,1)} %k_hbm.1, bf16[128,4096]{1,0:T(8,128)(2,1)} %v_hbm.1), custom_call_target="tpu_custom_call" | custom-call | tf_op jit(solution)/shard_map/scan_attention/pallas_call | solution.py:334
  24.1 0.0 copy-done
  24.1 1.1 %scale_rows.1 = bf16[128,4096]{1,0:T(8,128)(2,1)} custom-call(bf16[128,4096]{1,0:T(8,128)(2,1)S(1)} %get-tuple-element.7.att_ref, f32[128,128]{1,0:T(8,128)S(1)} %get-tuple-element.8.scale_ref, f32[1,4096]{1,0:T(1,128)S(1)} %bitcast.1), custom_call_target="tpu_custom_call" | custom-call | tf_op jit(solution)/shard_map/scale_rows/pallas_call | solution.py:365
Async XLA Ops:
  0.0 24.1 %copy-start = (f32[4096]{0:T(1024)S(1)}, f32[4096]{0:T(1024)}, u32[]{:S(2)}) copy-start(f32[4096]{0:T(1024)} %param.9) | copy-start | bytes 49156
where the time goes:
time: 25.3 us; the launch traced here: 25.2 us
  Pallas kernels  25.2 us (100%)
    pallas_call x1, Pallas kernels, per_device(): pl.pallas_call(functools.partial(kernel, nz, nh), out_shape=(jax.ShapeDty...  24.1 us
    pallas_call x1, Pallas kernels, per_device(): pl.pallas_call(functools.partial(scale_kernel, parts), out_shape=jax.Shap...  1.08 us

commit v1 on v0

--- a/solution.py
+++ b/solution.py
@@ -37,6 +37,9 @@
     pieces = own // ph
     docs = ends_ref.shape[0]
     chunk = 2 * rows
+    shard = nx * chunk
+    longest = nz * shard // nh
+    chained = longest > shard
     z = lax.axis_index("ctx")
     h = lax.axis_index("head")
     x = h // 2
@@ -187,7 +190,7 @@
         return carry
 
     steps = heads // unroll
-    pre = jnp.minimum(z * 4, steps)
+    pre = jnp.minimum(z * 4, steps) if chained else 0
     lax.fori_loop(0, pre, local_heads, 0)
 
     @pl.when(z == 0)
@@ -200,35 +203,41 @@
             device_id=device(x, c, z + 1), device_id_type=MESH)
 
     p_copies = {}
-    for p in range(pieces):
+
+    def fold(p):
         for s in range(nx - 1):
             t_copies[s, p].wait_recv()
-        add, whole = None, 1.0
+        add = None
         for xx in range(nx):
             got = tin[lax.rem(x + 2 * nx - 1 - xx, nx), p].astype(F32)
             add = got if xx == 0 else got + add * cont[xx]
-            whole = whole * cont[xx]
-            if xx < nx - 1:
-                partial[xx] = add
-        partial[nx - 1] = add
-
+            partial[p, xx] = add
+        if chained:
+            receive(p)
+            whole = 1.0
+            for xx in range(nx):
+                whole = whole * cont[xx]
+            add = add + zin[p].astype(F32) * whole
+        zout[p] = add.astype(BF16)
+
+        @pl.when(z < nz - 1)
+        def _():
+            z_copy(p).start()
+
+    def receive(p):
         @pl.when(z > 0)
         def _():
             z_copy(p).wait_recv()
 
+    def spread(p):
+        if not chained:
+            receive(p)
         carried = zin[p].astype(F32)
-        run = partial[nx - 1] + carried * whole
-        zout[p] = run.astype(BF16)
-
-        @pl.when(z < nz - 1)
-        def _():
-            z_copy(p).start()
-
         passed = 1.0
         prefix[0, p] = zin[p]
         for xx in range(nx - 1):
             passed = passed * cont[xx]
-            prefix[xx + 1, p] = (partial[xx] + carried * passed).astype(BF16)
+            prefix[xx + 1, p] = (partial[p, xx] + carried * passed).astype(BF16)
         for s in range(nx - 1):
             cp = pltpu.make_async_remote_copy(
                 src_ref=prefix.at[ahead[s], p], dst_ref=pin.at[s, p],
@@ -236,7 +245,15 @@
                 device_id=device(ahead[s], c), device_id_type=MESH)
             cp.start()
             p_copies[s, p] = cp
-        lax.fori_loop(pre + (steps - pre) * p // pieces, pre + (steps - pre) * (p + 1) // pieces, local_heads, 0)
+
+    lag = 0 if chained else min(3, pieces)
+    slots = pieces + lag
+    for slot in range(slots):
+        if slot < pieces:
+            fold(slot)
+        if slot >= lag:
+            spread(slot - lag)
+        lax.fori_loop(pre + (steps - pre) * slot // slots, pre + (steps - pre) * (slot + 1) // slots, local_heads, 0)
 
     a_copies = []
     total = jnp.zeros((rows, DH), F32)
@@ -345,7 +362,7 @@
             pltpu.VMEM((chunk, DH), F32),
             pltpu.VMEM((far, pieces, ph, DH, DH), BF16),
             pltpu.VMEM((nx, pieces, ph, DH, DH), BF16),
-            pltpu.VMEM((nx, ph, DH, DH), F32),
+            pltpu.VMEM((pieces, nx, ph, DH, DH), F32),
             pltpu.VMEM((nx, pieces, ph, DH, DH), BF16),
             pltpu.VMEM((far, pieces, ph, DH, DH), BF16),
             pltpu.VMEM((pieces, ph, DH, DH), BF16),

time: 25.3 us -> 21.6 us (0.85)
  the two profiles are of different devices: /device:TPU:29 before, /device:TPU:0 now
where the time goes in v1:
time: 21.6 us; the launch traced here: 21.4 us
  Pallas kernels  21.4 us (99%)
    pallas_call x1, Pallas kernels, per_device(): pl.pallas_call(functools.partial(kernel, nz, nh), out_shape=(jax.ShapeDty...  20.3 us
    pallas_call x1, Pallas kernels, per_device(): pl.pallas_call(functools.partial(scale_kernel, parts), out_shape=jax.Shap...  1.08 us

profile of v1, /device:TPU:0, one launch (start us, length us, event | category | flops | bytes accessed | tf_op | source)
XLA Modules:
  0.0 21.4 jit_solution(17884042479804708785)
XLA Ops:
  0.0 0.0 copy-start
  0.0 20.3 %scan_attention.1 = (bf16[128,4096]{1,0:T(8,128)(2,1)S(1)}, f32[128,128]{1,0:T(8,128)S(1)}) custom-call(s32[5]{0:T(128)} %docs_hbm.1, bf16[128,4096]{1,0:T(8,128)(2,1)} %q_hbm.1, bf16[128,4096]{1,0:T(8,128)(2,1)} %k_hbm.1, bf16[128,4096]{1,0:T(8,128)(2,1)} %v_hbm.1), custom_call_target="tpu_custom_call" | custom-call | tf_op jit(solution)/shard_map/scan_attention/pallas_call | solution.py:351
  20.3 0.0 copy-done
  20.3 1.1 %scale_rows.1 = bf16[128,4096]{1,0:T(8,128)(2,1)} custom-call(bf16[128,4096]{1,0:T(8,128)(2,1)S(1)} %get-tuple-element.7.att_ref, f32[128,128]{1,0:T(8,128)S(1)} %get-tuple-element.8.scale_ref, f32[1,4096]{1,0:T(1,128)S(1)} %bitcast.1), custom_call_target="tpu_custom_call" | custom-call | tf_op jit(solution)/shard_map/scale_rows/pallas_call | solution.py:382
Async XLA Ops:
  0.0 20.3 %copy-start = (f32[4096]{0:T(1024)S(1)}, f32[4096]{0:T(1024)}, u32[]{:S(2)}) copy-start(f32[4096]{0:T(1024)} %param.9) | copy-start | bytes 49156

commit v2 on v1

v2 whole, which is shorter than its diff:
```python
import functools

import jax
import jax.numpy as jnp
from jax import lax
from jax.experimental import pallas as pl
from jax.experimental.pallas import tpu as pltpu
from jax.sharding import PartitionSpec as P

DH = 128
MESH = pl.DeviceIdType.MESH
LIMIT1 = 52 << 20
LIMIT2 = 8 << 20
F32 = jnp.float32
BF16 = jnp.bfloat16
BATCH = 4


def silu(v):
    v = v.astype(F32)
    half = 0.5 * v
    return (half + half * jnp.tanh(half)).astype(BF16)


def kernel(nz, nh, group, docs_hbm, q_hbm, k_hbm, v_hbm, out_ref, scale_ref,
           ends_ref, doc_sem, qb, kb, vb, wq, maskb, joinb, keepb, tsend, tt, xout, tin, partial, zin, zout, prefix, pin, st, fin,
           load_sem, s_send, s_recv, t_send, t_recv, z_send, z_recv, p_send, p_recv, f_send, f_recv):
    nx = nh // 2
    rows, width = q_hbm.shape
    heads = width // DH
    half = heads // 2
    own = half // nx
    docs = ends_ref.shape[0]
    chunk = 2 * rows
    shard = nx * chunk
    longest = nz * shard // nh
    chained = longest > shard
    z = lax.axis_index("ctx")
    h = lax.axis_index("head")
    x = h // 2
    c = h % 2
    o = 1 - c

    def device(xx, cc, zz=None):
        return {"ctx": z if zz is None else zz, "head": 2 * xx + cc}

    ahead = [lax.rem(x + 1 + s, nx) for s in range(nx)]
    behind = [lax.rem(x + 2 * nx - 1 - s, nx) for s in range(nx)]

    barrier = pltpu.get_barrier_semaphore()
    pl.semaphore_signal(barrier, inc=1, device_id=device(x, o), device_id_type=MESH)
    for s in range(nx - 1):
        pl.semaphore_signal(barrier, inc=1, device_id=device(ahead[s], c), device_id_type=MESH)

    @pl.when(z > 0)
    def _():
        pl.semaphore_signal(barrier, inc=1, device_id=device(x, c, z - 1), device_id_type=MESH)

    @pl.when(z < nz - 1)
    def _():
        pl.semaphore_signal(barrier, inc=1, device_id=device(x, c, z + 1), device_id_type=MESH)

    docs_copy = pltpu.make_async_copy(docs_hbm, ends_ref, doc_sem)
    docs_copy.start()

    def cols(head, count=1):
        return pl.ds(pl.multiple_of(head * DH, DH), count * DH)

    def first_head(side, s, g):
        return (o if side else c) * half + ahead[s] * own + g * group

    groups = own // group

    def load(side, s, g, count, sem):
        at = cols(first_head(side, s, g), count)
        for src, dst in ((k_hbm, kb), (v_hbm, vb)):
            pltpu.make_async_copy(src.at[:, at], dst.at[:, at], load_sem.at[sem]).start()

    def loaded(sem, count):
        at = pl.ds(0, 4 * count * DH)
        pltpu.make_async_copy(k_hbm.at[:, at], kb.at[:, at], load_sem.at[sem]).wait()

    for side in (1, 0):
        load(side, 0, 0, group, 0)
    for s in range(nx):
        skip = 0 if s else 1
        if groups > skip:
            for side in (1, 0):
                load(side, s, skip, own - skip * group, s + 1)
    q_copy = pltpu.make_async_copy(q_hbm, qb, load_sem.at[nx + 1])
    q_copy.start()

    docs_copy.wait()
    ends = [ends_ref[0]]
    for d in range(1, docs):
        ends.append(ends[-1] + ends_ref[d])

    def seg_of(pos):
        total = jnp.where(pos < 0, -1, 0)
        for end in ends:
            total = total + jnp.where(pos >= end, 1, 0)
        return total

    def spans(start, count):
        return jnp.where(seg_of(start - 1) == seg_of(start + count - 1), 1.0, 0.0).astype(F32)

    shard_start = z * shard
    chip = shard_start + x * chunk
    first = chip + c * rows
    row_i = lax.broadcasted_iota(jnp.int32, (rows, DH), 0)
    seg_r = seg_of(row_i + first)
    joinb[...] = jnp.where(seg_r == seg_of(first - 1), 1.0, 0.0).astype(BF16)
    keepb[...] = jnp.where(seg_r == seg_of(first + rows - 1), 1.0, 0.0).astype(BF16)
    col_i = lax.broadcasted_iota(jnp.int32, (8, rows), 1)
    seg_c = seg_of(col_i + first)[0:1]
    for g in range(rows // DH):
        sc = jnp.broadcast_to(seg_c[:, g * DH:(g + 1) * DH], (rows, DH))
        ci = lax.broadcasted_iota(jnp.int32, (rows, DH), 1) + g * DH
        maskb[:, g * DH:(g + 1) * DH] = jnp.where((seg_r == sc) & (row_i >= ci), 1.0, 0.0).astype(BF16)
    low = spans(chip, rows)
    high = spans(chip + rows, rows)
    cont = [spans(shard_start + xx * chunk, chunk) for xx in range(nx)]

    def tails(s, g):
        if s == 0 and g == 0:
            loaded(0, group)
        elif s == 0 and g == 1:
            loaded(1, own - group)
        elif g == 0:
            loaded(s + 1, own)
        for i in range(group):
            for side in (1, 0):
                at = cols(first_head(side, s, g) + i)
                kk = silu(kb[:, at])
                kb[:, at] = kk
                t = lax.dot_general(kk * keepb[...], vb[:, at], (((0,), (0,)), ((), ())), preferred_element_type=F32).astype(BF16)
                if side:
                    tsend[s, g * group + i] = t
                else:
                    tt[c, s, g * group + i] = t

    s_copies = {}

    def pass_tails(s, g):
        at = pl.ds(g * group, group)
        cp = pltpu.make_async_remote_copy(
            src_ref=tsend.at[s, at], dst_ref=tt.at[c, s, at], send_sem=s_send, recv_sem=s_recv.at[s, g],
            device_id=device(x, o), device_id_type=MESH)
        cp.start()
        s_copies[s, g] = cp

    t_copies = {}

    def join_tails(s, g):
        s_copies[s, g].wait_recv()
        for i in range(group):
            p = g * group + i
            t = (tt[1, s, p].astype(F32) + tt[0, s, p].astype(F32) * high).astype(BF16)
            if s == nx - 1:
                tin[s, p] = t
                continue
            xout[s, p] = t
            cp = pltpu.make_async_remote_copy(
                src_ref=xout.at[s, p], dst_ref=tin.at[s, p], send_sem=t_send, recv_sem=t_recv.at[s, p],
                device_id=device(ahead[s], c), device_id_type=MESH)
            cp.start()
            t_copies[s, p] = cp

    tails(0, 0)
    pl.semaphore_wait(barrier, nx + jnp.where(z > 0, 1, 0) + jnp.where(z < nz - 1, 1, 0))
    pass_tails(0, 0)
    order = [(s, g) for s in range(nx) for g in range(groups)]
    delay = min(3, len(order) - 1)
    for n, (s, g) in enumerate(order):
        if n:
            tails(s, g)
            pass_tails(s, g)
        if n >= delay:
            join_tails(*order[n - delay])
    for s, g in order[len(order) - delay:]:
        join_tails(s, g)

    q_copy.wait()

    def head_of(side, s, p):
        owner = x if s == nx - 1 else behind[s]
        return (o if side else c) * half + owner * own + p

    def local(batch):
        for one in batch:
            head = head_of(*one)
            qq = silu(qb[:, cols(head)])
            scores = lax.dot_general(qq, kb[:, cols(head)], (((1,), (1,)), ((), ())), preferred_element_type=F32)
            wq[head, :, :rows] = scores.astype(BF16) * maskb[...]
            wq[head, :, rows:] = qq * joinb[...]

    @pl.when(z == 0)
    def _():
        zin[...] = jnp.zeros_like(zin)

    def z_copy(p):
        return pltpu.make_async_remote_copy(
            src_ref=zout.at[p], dst_ref=zin.at[p], send_sem=z_send, recv_sem=z_recv.at[p],
            device_id=device(x, c, z + 1), device_id_type=MESH)

    def receive(p):
        @pl.when(z > 0)
        def _():
            z_copy(p).wait_recv()

    def fold(p):
        for s in range(nx - 1):
            t_copies[s, p].wait_recv()
        add = None
        for xx in range(nx):
            got = tin[lax.rem(x + 2 * nx - 1 - xx, nx), p].astype(F32)
            add = got if xx == 0 else got + add * cont[xx]
            partial[p, xx] = add
        if chained:
            receive(p)
            whole = 1.0
            for xx in range(nx):
                whole = whole * cont[xx]
            add = add + zin[p].astype(F32) * whole
        zout[p] = add.astype(BF16)

        @pl.when(z < nz - 1)
        def _():
            z_copy(p).start()

    p_copies = {}
    f_copies = {}

    def forward(s, p, state):
        into = tt[0, nx - 1 if s == nx - 1 else nx - 2 - s, p].astype(F32) + state.astype(F32) * low
        st[0, s, p] = state
        st[1, s, p] = into.astype(BF16)
        cp = pltpu.make_async_remote_copy(
            src_ref=st.at[o, s, p], dst_ref=fin.at[s, p], send_sem=f_send, recv_sem=f_recv.at[s, p],
            device_id=device(x, o), device_id_type=MESH)
        cp.start()
        f_copies[s, p] = cp

    def spread(p):
        if not chained:
            receive(p)
        carried = zin[p].astype(F32)
        passed = 1.0
        prefix[0, p] = zin[p]
        for xx in range(nx - 1):
            passed = passed * cont[xx]
            prefix[xx + 1, p] = (partial[p, xx] + carried * passed).astype(BF16)
        for s in range(nx - 1):
            cp = pltpu.make_async_remote_copy(
                src_ref=prefix.at[ahead[s], p], dst_ref=pin.at[s, p],
                send_sem=p_send, recv_sem=p_recv.at[s, p],
                device_id=device(ahead[s], c), device_id_type=MESH)
            cp.start()
            p_copies[s, p] = cp
        forward(nx - 1, p, prefix[x, p])

    def finish(batch, total):
        for side, s, p in batch:
            if side:
                f_copies[s, p].wait_recv()
        for side, s, p in batch:
            head = head_of(side, s, p)
            state = fin[s, p] if side else st[c, s, p]
            both = jnp.concatenate([vb[:, cols(head)], state], axis=0)
            att = jnp.dot(wq[head], both, preferred_element_type=F32).astype(BF16)
            out_ref[:, cols(head)] = att
            att = att.astype(F32)
            total = total + att * att
        return total

    lag = 0 if chained else min(3, own)
    rest = [(s, p) for s in range(nx - 1) for p in range(own)]
    every = [(side, s, p) for s, p in [(nx - 1, p) for p in range(own)] + rest for side in (0, 1)]
    ready = {}
    for n in range(own):
        ready[0, nx - 1, n] = n + lag
        ready[1, nx - 1, n] = n + lag + 2
    for n, (s, p) in enumerate(rest):
        ready[0, s, p] = n + own
        ready[1, s, p] = n + own + 2
    slots = own + len(rest)
    waiting = sorted(ready, key=lambda one: (ready[one], one))
    todo = list(every)
    total = jnp.zeros((rows, DH), F32)
    for slot in range(slots):
        if slot < own:
            fold(slot)
        if lag <= slot < own + lag:
            spread(slot - lag)
        if slot >= own:
            s, p = rest[slot - own]
            p_copies[s, p].wait_recv()
            forward(s, p, pin[s, p])
        count = -(-len(todo) // max(own - slot, 1))
        local(todo[:count])
        todo = todo[count:]
        now = [one for one in waiting if ready[one] <= slot and one not in todo]
        if len(now) >= BATCH:
            total = finish(now[:BATCH], total)
            waiting = [one for one in waiting if one not in now[:BATCH]]
    while waiting:
        total = finish(waiting[:2], total)
        waiting = waiting[2:]
    scale = lax.rsqrt(jnp.sum(total, axis=1, keepdims=True) / width + 1e-05)
    scale_ref[...] = jnp.broadcast_to(scale, (rows, DH))

    def sent(src, dst, sem, recv):
        pltpu.make_async_remote_copy(
            src_ref=src, dst_ref=dst, send_sem=sem, recv_sem=recv,
            device_id=device(x, o), device_id_type=MESH).wait_send()

    sent(tsend, tt.at[c], s_send, s_recv.at[0, 0])
    if nx > 1:
        sent(xout, xout, t_send, t_recv.at[0, 0])
        sent(pin, pin, p_send, p_recv.at[0, 0])
    sent(st.at[o], fin, f_send, f_recv.at[0, 0])

    @pl.when(z < nz - 1)
    def _():
        sent(zout, zin, z_send, z_recv.at[0])


def scale_kernel(parts, att_ref, scale_ref, gain_ref, out_hbm, buf, sems):
    rows, width = att_ref.shape
    part = width // parts
    scale = scale_ref[...]
    copies = []
    for j in range(parts):
        for i in range(part // DH):
            at = j * part + i * DH
            v = att_ref[:, at:at + DH].astype(F32)
            buf[j, :, i * DH:(i + 1) * DH] = (v * scale * gain_ref[0:1, at:at + DH]).astype(BF16)
        cp = pltpu.make_async_copy(buf.at[j], out_hbm.at[:, j * part:(j + 1) * part], sems.at[j])
        cp.start()
        copies.append(cp)
    for cp in copies:
        cp.wait()


def per_device(nz, nh, queries, keys_in, values, doc_lengths, rms_gain):
    rows, width = queries.shape
    nx = nh // 2
    heads = width // DH
    own = heads // 2 // nx
    group = 2 if own % 2 == 0 else 1
    groups = own // group
    far = max(nx - 1, 1)
    docs = doc_lengths.shape
    vmem = pltpu.VMEM
    full = vmem((rows, width), BF16)
    dma = pltpu.SemaphoreType.DMA
    hbm_spec = pl.BlockSpec(memory_space=pltpu.HBM)
    vmem_spec = pl.BlockSpec(memory_space=pltpu.VMEM)
    attended, scale = pl.pallas_call(
        functools.partial(kernel, nz, nh, group),
        out_shape=(jax.ShapeDtypeStruct((rows, width), BF16), jax.ShapeDtypeStruct((rows, DH), F32)),
        in_specs=[hbm_spec] * 4,
        out_specs=(vmem_spec, vmem_spec),
        scratch_shapes=[
            pltpu.SMEM(docs, jnp.int32), dma(()),
            full, full, full,
            vmem((heads, rows, rows + DH), BF16),
            vmem((rows, rows), BF16),
            vmem((rows, DH), BF16),
            vmem((rows, DH), BF16),
            vmem((nx, own, DH, DH), BF16),
            vmem((2, nx, own, DH, DH), BF16),
            vmem((far, own, DH, DH), BF16),
            vmem((nx, own, DH, DH), BF16),
            vmem((own, nx, DH, DH), F32),
            vmem((own, DH, DH), BF16),
            vmem((own, DH, DH), BF16),
            vmem((nx, own, DH, DH), BF16),
            vmem((far, own, DH, DH), BF16),
            vmem((2, nx, own, DH, DH), BF16),
            vmem((nx, own, DH, DH), BF16),
            dma((nx + 2,)),
            dma(()), dma((nx, groups)),
            dma(()), dma((far, own)),
            dma(()), dma((own,)),
            dma(()), dma((far, own)),
            dma(()), dma((nx, own)),
        ],
        compiler_params=pltpu.CompilerParams(collective_id=0, has_side_effects=True, vmem_limit_bytes=LIMIT1),
        name="scan_attention",
    )(pltpu.with_memory_space_constraint(doc_lengths, pltpu.HBM), queries, keys_in, values)
    parts = 4
    return pl.pallas_call(
        functools.partial(scale_kernel, parts),
        out_shape=jax.ShapeDtypeStruct((rows, width), BF16),
        in_specs=[pl.BlockSpec(memory_space=pltpu.VMEM)] * 3,
        out_specs=pl.BlockSpec(memory_space=pl.ANY),
        scratch_shapes=[pltpu.VMEM((parts, rows, width // parts), BF16), dma((parts,))],
        compiler_params=pltpu.CompilerParams(vmem_limit_bytes=LIMIT2),
        name="scale_rows",
    )(attended, scale, rms_gain.reshape(1, width))


def solution(mesh):
    split = P(("groups", "ctx", "head"), None)
    return jax.shard_map(
        functools.partial(per_device, mesh.shape["ctx"], mesh.shape["head"]),
        mesh=mesh,
        in_specs=(split, split, split, P("groups"), P()),
        out_specs=split,
        check_vma=False,
    )
```

time: 21.6 us -> 20.7 us (0.958)
  the two profiles are of different devices: /device:TPU:0 before, /device:TPU:1 now
where the time goes in v2:
time: 20.7 us; the launch traced here: 20.5 us
  Pallas kernels  20.5 us (99%)
    pallas_call x1, Pallas kernels, per_device(): pl.pallas_call(functools.partial(kernel, nz, nh, group), out_shape=(jax.S...  19.4 us
    pallas_call x1, Pallas kernels, per_device(): pl.pallas_call(functools.partial(scale_kernel, parts), out_shape=jax.Shap...  1.08 us

profile of v2, /device:TPU:1, one launch (start us, length us, event | category | flops | bytes accessed | tf_op | source)
XLA Modules:
  0.0 20.5 jit_solution(17058965650821151891)
XLA Ops:
  0.0 0.0 copy-start
  0.0 19.4 %scan_attention.1 = (bf16[128,4096]{1,0:T(8,128)(2,1)S(1)}, f32[128,128]{1,0:T(8,128)S(1)}) custom-call(s32[5]{0:T(128)} %docs_hbm.1, bf16[128,4096]{1,0:T(8,128)(2,1)} %q_hbm.1, bf16[128,4096]{1,0:T(8,128)(2,1)} %k_hbm.1, bf16[128,4096]{1,0:T(8,128)(2,1)} %v_hbm.1), custom_call_target="tpu_custom_call" | custom-call | tf_op jit(solution)/shard_map/scan_attention/pallas_call | solution.py:359
  19.4 0.0 copy-done
  19.4 1.1 %scale_rows.1 = bf16[128,4096]{1,0:T(8,128)(2,1)} custom-call(bf16[128,4096]{1,0:T(8,128)(2,1)S(1)} %get-tuple-element.7.att_ref, f32[128,128]{1,0:T(8,128)S(1)} %get-tuple-element.8.scale_ref, f32[1,4096]{1,0:T(1,128)S(1)} %bitcast.1), custom_call_target="tpu_custom_call" | custom-call | tf_op jit(solution)/shard_map/scale_rows/pallas_call | solution.py:393
Async XLA Ops:
  0.0 19.4 %copy-start = (f32[4096]{0:T(1024)S(1)}, f32[4096]{0:T(1024)}, u32[]{:S(2)}) copy-start(f32[4096]{0:T(1024)} %param.9) | copy-start | bytes 49156

commit v3 on v2

--- a/solution.py
+++ b/solution.py
@@ -23,8 +23,8 @@
 
 
 def kernel(nz, nh, group, docs_hbm, q_hbm, k_hbm, v_hbm, out_ref, scale_ref,
-           ends_ref, doc_sem, qb, kb, vb, wq, maskb, joinb, keepb, tsend, tt, xout, tin, partial, zin, zout, prefix, pin, st, fin,
-           load_sem, s_send, s_recv, t_send, t_recv, z_send, z_recv, p_send, p_recv, f_send, f_recv):
+           ends_ref, doc_sem, qb, kb, vb, wq, maskb, joinb, keepb, tsend, tt, xout, tin, partial, zin, zout, prefix, pin, st, fin, early,
+           load_sem, s_send, s_recv, t_send, t_recv, z_send, z_recv, p_send, p_recv, f_send, f_recv, e_send, e_recv):
     nx = nh // 2
     rows, width = q_hbm.shape
     heads = width // DH
@@ -52,6 +52,10 @@
     for s in range(nx - 1):
         pl.semaphore_signal(barrier, inc=1, device_id=device(ahead[s], c), device_id_type=MESH)
 
+    across = [ahead[0], behind[0]][:min(nx - 1, 2)]
+    for xx in across:
+        pl.semaphore_signal(barrier, inc=1, device_id=device(xx, o), device_id_type=MESH)
+
     @pl.when(z > 0)
     def _():
         pl.semaphore_signal(barrier, inc=1, device_id=device(x, c, z - 1), device_id_type=MESH)
@@ -59,9 +63,6 @@
     @pl.when(z < nz - 1)
     def _():
         pl.semaphore_signal(barrier, inc=1, device_id=device(x, c, z + 1), device_id_type=MESH)
-
-    docs_copy = pltpu.make_async_copy(docs_hbm, ends_ref, doc_sem)
-    docs_copy.start()
 
     def cols(head, count=1):
         return pl.ds(pl.multiple_of(head * DH, DH), count * DH)
@@ -82,6 +83,8 @@
 
     for side in (1, 0):
         load(side, 0, 0, group, 0)
+    docs_copy = pltpu.make_async_copy(docs_hbm, ends_ref, doc_sem)
+    docs_copy.start()
     for s in range(nx):
         skip = 0 if s else 1
         if groups > skip:
@@ -90,6 +93,14 @@
     q_copy = pltpu.make_async_copy(q_hbm, qb, load_sem.at[nx + 1])
     q_copy.start()
 
+    def activate(s, g):
+        for i in range(group):
+            for side in (1, 0):
+                at = cols(first_head(side, s, g) + i)
+                kb[:, at] = silu(kb[:, at])
+
+    loaded(0, group)
+    activate(0, 0)
     docs_copy.wait()
     ends = [ends_ref[0]]
     for d in range(1, docs):
@@ -119,19 +130,18 @@
         maskb[:, g * DH:(g + 1) * DH] = jnp.where((seg_r == sc) & (row_i >= ci), 1.0, 0.0).astype(BF16)
     low = spans(chip, rows)
     high = spans(chip + rows, rows)
+    other = spans(shard_start + behind[0] * chunk + rows, rows)
     cont = [spans(shard_start + xx * chunk, chunk) for xx in range(nx)]
 
     def tails(s, g):
-        if s == 0 and g == 0:
-            loaded(0, group)
-        elif s == 0 and g == 1:
+        if s == 0 and g == 1:
             loaded(1, own - group)
-        elif g == 0:
+        elif s and g == 0:
             loaded(s + 1, own)
         for i in range(group):
             for side in (1, 0):
                 at = cols(first_head(side, s, g) + i)
-                kk = silu(kb[:, at])
+                kk = kb[:, at] if s == 0 and g == 0 else silu(kb[:, at])
                 kb[:, at] = kk
                 t = lax.dot_general(kk * keepb[...], vb[:, at], (((0,), (0,)), ((), ())), preferred_element_type=F32).astype(BF16)
                 if side:
@@ -155,19 +165,29 @@
         s_copies[s, g].wait_recv()
         for i in range(group):
             p = g * group + i
+            if s == 0 and p == 0 and nx > 1:
+                continue
             t = (tt[1, s, p].astype(F32) + tt[0, s, p].astype(F32) * high).astype(BF16)
             if s == nx - 1:
                 tin[s, p] = t
                 continue
-            xout[s, p] = t
+            xout[s * own + p] = t
             cp = pltpu.make_async_remote_copy(
-                src_ref=xout.at[s, p], dst_ref=tin.at[s, p], send_sem=t_send, recv_sem=t_recv.at[s, p],
+                src_ref=xout.at[s * own + p], dst_ref=tin.at[s, p], send_sem=t_send, recv_sem=t_recv.at[s, p],
                 device_id=device(ahead[s], c), device_id_type=MESH)
             cp.start()
             t_copies[s, p] = cp
 
     tails(0, 0)
-    pl.semaphore_wait(barrier, nx + jnp.where(z > 0, 1, 0) + jnp.where(z < nz - 1, 1, 0))
+    pl.semaphore_wait(barrier, nx + len(across) + jnp.where(z > 0, 1, 0) + jnp.where(z < nz - 1, 1, 0))
+    e_copies = []
+    if nx > 1:
+        for n, (src, cc) in enumerate(((tt.at[c, 0, 0], c), (tsend.at[0, 0], o))):
+            cp = pltpu.make_async_remote_copy(
+                src_ref=src, dst_ref=early.at[c], send_sem=e_send, recv_sem=e_recv.at[n],
+                device_id=device(ahead[0], cc), device_id_type=MESH)
+            cp.start()
+            e_copies.append(cp)
     pass_tails(0, 0)
     order = [(s, g) for s in range(nx) for g in range(groups)]
     delay = min(3, len(order) - 1)
@@ -198,6 +218,10 @@
     def _():
         zin[...] = jnp.zeros_like(zin)
 
+    @pl.when((z == 0) & (x == 0))
+    def _():
+        pin[...] = jnp.zeros_like(pin)
+
     def z_copy(p):
         return pltpu.make_async_remote_copy(
             src_ref=zout.at[p], dst_ref=zin.at[p], send_sem=z_send, recv_sem=z_recv.at[p],
@@ -210,6 +234,11 @@
 
     def fold(p):
         for s in range(nx - 1):
+            if s == 0 and p == 0:
+                for cp in e_copies:
+                    cp.wait_recv()
+                tin[0, 0] = (early[1].astype(F32) + early[0].astype(F32) * other).astype(BF16)
+                continue
             t_copies[s, p].wait_recv()
         add = None
         for xx in range(nx):
@@ -252,10 +281,10 @@
             prefix[xx + 1, p] = (partial[p, xx] + carried * passed).astype(BF16)
         for s in range(nx - 1):
             cp = pltpu.make_async_remote_copy(
-                src_ref=prefix.at[ahead[s], p], dst_ref=pin.at[s, p],
+                src_ref=prefix.at[ahead[s], p], dst_ref=pin.at[s * own + p],
                 send_sem=p_send, recv_sem=p_recv.at[s, p],
                 device_id=device(ahead[s], c), device_id_type=MESH)
-            cp.start()
+            pl.when((z > 0) | (ahead[s] > 0))(cp.start)
             p_copies[s, p] = cp
         forward(nx - 1, p, prefix[x, p])
 
@@ -294,8 +323,8 @@
             spread(slot - lag)
         if slot >= own:
             s, p = rest[slot - own]
-            p_copies[s, p].wait_recv()
-            forward(s, p, pin[s, p])
+            pl.when((z > 0) | (x > 0))(p_copies[s, p].wait_recv)
+            forward(s, p, pin[s * own + p])
         count = -(-len(todo) // max(own - slot, 1))
         local(todo[:count])
         todo = todo[count:]
@@ -316,8 +345,20 @@
 
     sent(tsend, tt.at[c], s_send, s_recv.at[0, 0])
     if nx > 1:
-        sent(xout, xout, t_send, t_recv.at[0, 0])
-        sent(pin, pin, p_send, p_recv.at[0, 0])
+        sent(early, early, e_send, e_recv.at[0])
+        late = pl.ds(1, (nx - 1) * own - 1)
+        sent(xout.at[late], xout.at[late], t_send, t_recv.at[0, 0])
+
+        @pl.when((z > 0) | (x == 0))
+        def _():
+            sent(pin, pin, p_send, p_recv.at[0, 0])
+
+    if nx > 2:
+        @pl.when((z == 0) & (x > 0))
+        def _():
+            most = pl.ds(0, (nx - 2) * own)
+            sent(pin.at[most], pin.at[most], p_send, p_recv.at[0, 0])
+
     sent(st.at[o], fin, f_send, f_recv.at[0, 0])
 
     @pl.when(z < nz - 1)
@@ -370,21 +411,23 @@
             vmem((rows, DH), BF16),
             vmem((nx, own, DH, DH), BF16),
             vmem((2, nx, own, DH, DH), BF16),
-            vmem((far, own, DH, DH), BF16),
+            vmem((far * own, DH, DH), BF16),
             vmem((nx, own, DH, DH), BF16),
             vmem((own, nx, DH, DH), F32),
             vmem((own, DH, DH), BF16),
             vmem((own, DH, DH), BF16),
             vmem((nx, own, DH, DH), BF16),
-            vmem((far, own, DH, DH), BF16),
+            vmem((far * own, DH, DH), BF16),
             vmem((2, nx, own, DH, DH), BF16),
             vmem((nx, own, DH, DH), BF16),
+            vmem((2, DH, DH), BF16),
             dma((nx + 2,)),
             dma(()), dma((nx, groups)),
             dma(()), dma((far, own)),
             dma(()), dma((own,)),
             dma(()), dma((far, own)),
             dma(()), dma((nx, own)),
+            dma(()), dma((2,)),
         ],
         compiler_params=pltpu.CompilerParams(collective_id=0, has_side_effects=True, vmem_limit_bytes=LIMIT1),
         name="scan_attention",

time: 20.7 us -> 19.3 us (0.932)
  the two profiles are of different devices: /device:TPU:1 before, /device:TPU:9 now
where the time goes in v3:
time: 19.3 us; the launch traced here: 19.2 us
  Pallas kernels  19.1 us (99%)
    pallas_call x1, Pallas kernels, per_device(): pl.pallas_call(functools.partial(kernel, nz, nh, group), out_shape=(jax.S...  18.1 us
    pallas_call x1, Pallas kernels, per_device(): pl.pallas_call(functools.partial(scale_kernel, parts), out_shape=jax.Shap...  1.08 us

profile of v3, /device:TPU:9, one launch (start us, length us, event | category | flops | bytes accessed | tf_op | source)
XLA Modules:
  0.0 19.2 jit_solution(15223587376711392001)
XLA Ops:
  0.0 0.0 copy-start
  0.0 18.1 %scan_attention.1 = (bf16[128,4096]{1,0:T(8,128)(2,1)S(1)}, f32[128,128]{1,0:T(8,128)S(1)}) custom-call(s32[5]{0:T(128)} %docs_hbm.1, bf16[128,4096]{1,0:T(8,128)(2,1)} %q_hbm.1, bf16[128,4096]{1,0:T(8,128)(2,1)} %k_hbm.1, bf16[128,4096]{1,0:T(8,128)(2,1)} %v_hbm.1), custom_call_target="tpu_custom_call" | custom-call | tf_op jit(solution)/shard_map/scan_attention/pallas_call | solution.py:400
  18.1 0.0 copy-done
  18.1 1.1 %scale_rows.1 = bf16[128,4096]{1,0:T(8,128)(2,1)} custom-call(bf16[128,4096]{1,0:T(8,128)(2,1)S(1)} %get-tuple-element.7.att_ref, f32[128,128]{1,0:T(8,128)S(1)} %get-tuple-element.8.scale_ref, f32[1,4096]{1,0:T(1,128)S(1)} %bitcast.1), custom_call_target="tpu_custom_call" | custom-call | tf_op jit(solution)/shard_map/scale_rows/pallas_call | solution.py:436
Async XLA Ops:
  0.0 18.1 %copy-start = (f32[4096]{0:T(1024)S(1)}, f32[4096]{0:T(1024)}, u32[]{:S(2)}) copy-start(f32[4096]{0:T(1024)} %param.9) | copy-start | bytes 49156

commit v4 on v3

--- a/solution.py
+++ b/solution.py
@@ -14,6 +14,8 @@
 F32 = jnp.float32
 BF16 = jnp.bfloat16
 BATCH = 4
+SKIP = 0
+LATE = 4
 
 
 def silu(v):
@@ -24,7 +26,7 @@
 
 def kernel(nz, nh, group, docs_hbm, q_hbm, k_hbm, v_hbm, out_ref, scale_ref,
            ends_ref, doc_sem, qb, kb, vb, wq, maskb, joinb, keepb, tsend, tt, xout, tin, partial, zin, zout, prefix, pin, st, fin, early,
-           load_sem, s_send, s_recv, t_send, t_recv, z_send, z_recv, p_send, p_recv, f_send, f_recv, e_send, e_recv):
+           load_sem, s_send, s_recv, t_send, t_recv, z_send, z_recv, p_send, p_recv, f_send, f_recv, e_send, e_recv, d_send):
     nx = nh // 2
     rows, width = q_hbm.shape
     heads = width // DH
@@ -35,6 +37,7 @@
     shard = nx * chunk
     longest = nz * shard // nh
     chained = longest > shard
+    skip = SKIP if nx == 2 and not chained else 0
     z = lax.axis_index("ctx")
     h = lax.axis_index("head")
     x = h // 2
@@ -47,11 +50,44 @@
     ahead = [lax.rem(x + 1 + s, nx) for s in range(nx)]
     behind = [lax.rem(x + 2 * nx - 1 - s, nx) for s in range(nx)]
 
+    def cols(head, count=1):
+        return pl.ds(pl.multiple_of(head * DH, DH), count * DH)
+
+    def first_head(side, s, g):
+        return (o if side else c) * half + ahead[s] * own + g * group
+
+    groups = own // group
+
+    tails_used = (z < nz - 1) | (x < nx - 1)
+
+    def load(side, s, g, count, sem):
+        at = cols(first_head(side, s, g), count)
+        for src, dst in ((k_hbm, kb), (v_hbm, vb)):
+            pltpu.make_async_copy(src.at[:, at], dst.at[:, at], load_sem.at[sem]).start()
+
+    def loaded(sem, count):
+        at = pl.ds(0, 4 * count * DH)
+        pltpu.make_async_copy(k_hbm.at[:, at], kb.at[:, at], load_sem.at[sem]).wait()
+
+    for side in (1, 0):
+        load(side, 0, 0, group, 0)
+    docs_copy = pltpu.make_async_copy(docs_hbm, ends_ref, doc_sem)
+    docs_copy.start()
+
     barrier = pltpu.get_barrier_semaphore()
     pl.semaphore_signal(barrier, inc=1, device_id=device(x, o), device_id_type=MESH)
     for s in range(nx - 1):
         pl.semaphore_signal(barrier, inc=1, device_id=device(ahead[s], c), device_id_type=MESH)
 
+    if skip:
+        @pl.when((x == 0) & (z > 0))
+        def _():
+            pl.semaphore_signal(barrier, inc=1, device_id=device(1, c, z - 1), device_id_type=MESH)
+
+        @pl.when((x > 0) & (z < nz - 1))
+        def _():
+            pl.semaphore_signal(barrier, inc=1, device_id=device(0, c, z + 1), device_id_type=MESH)
+
     across = [ahead[0], behind[0]][:min(nx - 1, 2)]
     for xx in across:
         pl.semaphore_signal(barrier, inc=1, device_id=device(xx, o), device_id_type=MESH)
@@ -64,27 +100,6 @@
     def _():
         pl.semaphore_signal(barrier, inc=1, device_id=device(x, c, z + 1), device_id_type=MESH)
 
-    def cols(head, count=1):
-        return pl.ds(pl.multiple_of(head * DH, DH), count * DH)
-
-    def first_head(side, s, g):
-        return (o if side else c) * half + ahead[s] * own + g * group
-
-    groups = own // group
-
-    def load(side, s, g, count, sem):
-        at = cols(first_head(side, s, g), count)
-        for src, dst in ((k_hbm, kb), (v_hbm, vb)):
-            pltpu.make_async_copy(src.at[:, at], dst.at[:, at], load_sem.at[sem]).start()
-
-    def loaded(sem, count):
-        at = pl.ds(0, 4 * count * DH)
-        pltpu.make_async_copy(k_hbm.at[:, at], kb.at[:, at], load_sem.at[sem]).wait()
-
-    for side in (1, 0):
-        load(side, 0, 0, group, 0)
-    docs_copy = pltpu.make_async_copy(docs_hbm, ends_ref, doc_sem)
-    docs_copy.start()
     for s in range(nx):
         skip = 0 if s else 1
         if groups > skip:
@@ -120,18 +135,7 @@
     first = chip + c * rows
     row_i = lax.broadcasted_iota(jnp.int32, (rows, DH), 0)
     seg_r = seg_of(row_i + first)
-    joinb[...] = jnp.where(seg_r == seg_of(first - 1), 1.0, 0.0).astype(BF16)
     keepb[...] = jnp.where(seg_r == seg_of(first + rows - 1), 1.0, 0.0).astype(BF16)
-    col_i = lax.broadcasted_iota(jnp.int32, (8, rows), 1)
-    seg_c = seg_of(col_i + first)[0:1]
-    for g in range(rows // DH):
-        sc = jnp.broadcast_to(seg_c[:, g * DH:(g + 1) * DH], (rows, DH))
-        ci = lax.broadcasted_iota(jnp.int32, (rows, DH), 1) + g * DH
-        maskb[:, g * DH:(g + 1) * DH] = jnp.where((seg_r == sc) & (row_i >= ci), 1.0, 0.0).astype(BF16)
-    low = spans(chip, rows)
-    high = spans(chip + rows, rows)
-    other = spans(shard_start + behind[0] * chunk + rows, rows)
-    cont = [spans(shard_start + xx * chunk, chunk) for xx in range(nx)]
 
     def tails(s, g):
         if s == 0 and g == 1:
@@ -175,20 +179,32 @@
             cp = pltpu.make_async_remote_copy(
                 src_ref=xout.at[s * own + p], dst_ref=tin.at[s, p], send_sem=t_send, recv_sem=t_recv.at[s, p],
                 device_id=device(ahead[s], c), device_id_type=MESH)
-            cp.start()
+            pl.when(tails_used)(cp.start)
             t_copies[s, p] = cp
 
     tails(0, 0)
-    pl.semaphore_wait(barrier, nx + len(across) + jnp.where(z > 0, 1, 0) + jnp.where(z < nz - 1, 1, 0))
+    pl.semaphore_wait(barrier, nx + len(across) + jnp.where(z > 0, 2 - x if skip else 1, 0) + jnp.where(z < nz - 1, 1 + x if skip else 1, 0))
     e_copies = []
     if nx > 1:
         for n, (src, cc) in enumerate(((tt.at[c, 0, 0], c), (tsend.at[0, 0], o))):
             cp = pltpu.make_async_remote_copy(
                 src_ref=src, dst_ref=early.at[c], send_sem=e_send, recv_sem=e_recv.at[n],
                 device_id=device(ahead[0], cc), device_id_type=MESH)
-            cp.start()
+            pl.when(tails_used)(cp.start)
             e_copies.append(cp)
     pass_tails(0, 0)
+    joinb[...] = jnp.where(seg_r == seg_of(first - 1), 1.0, 0.0).astype(BF16)
+    col_i = lax.broadcasted_iota(jnp.int32, (8, rows), 1)
+    seg_c = seg_of(col_i + first)[0:1]
+    for g in range(rows // DH):
+        sc = jnp.broadcast_to(seg_c[:, g * DH:(g + 1) * DH], (rows, DH))
+        ci = lax.broadcasted_iota(jnp.int32, (rows, DH), 1) + g * DH
+        maskb[:, g * DH:(g + 1) * DH] = jnp.where((seg_r == sc) & (row_i >= ci), 1.0, 0.0).astype(BF16)
+    low = spans(chip, rows)
+    high = spans(chip + rows, rows)
+    other = spans(shard_start + behind[0] * chunk + rows, rows)
+    cont = [spans(shard_start + xx * chunk, chunk) for xx in range(nx)]
+
     order = [(s, g) for s in range(nx) for g in range(groups)]
     delay = min(3, len(order) - 1)
     for n, (s, g) in enumerate(order):
@@ -234,12 +250,13 @@
 
     def fold(p):
         for s in range(nx - 1):
+            coming = (z < nz - 1) | (behind[s] < nx - 1)
             if s == 0 and p == 0:
                 for cp in e_copies:
-                    cp.wait_recv()
+                    pl.when(coming)(cp.wait_recv)
                 tin[0, 0] = (early[1].astype(F32) + early[0].astype(F32) * other).astype(BF16)
                 continue
-            t_copies[s, p].wait_recv()
+            pl.when(coming)(t_copies[s, p].wait_recv)
         add = None
         for xx in range(nx):
             got = tin[lax.rem(x + 2 * nx - 1 - xx, nx), p].astype(F32)
@@ -257,6 +274,15 @@
         def _():
             z_copy(p).start()
 
+        if p >= own - skip * (nz - 2):
+            cp = pltpu.make_async_remote_copy(
+                src_ref=zout.at[p], dst_ref=pin.at[p], send_sem=d_send.at[own - 1 - p], recv_sem=p_recv.at[0, p],
+                device_id=device(0, c, z + 1), device_id_type=MESH)
+            cond = (x > 0) & (p >= own - skip * (nz - 2 - z))
+            pl.when(cond)(cp.start)
+            skips.append((cp, cond))
+
+    skips = []
     p_copies = {}
     f_copies = {}
 
@@ -284,7 +310,7 @@
                 src_ref=prefix.at[ahead[s], p], dst_ref=pin.at[s * own + p],
                 send_sem=p_send, recv_sem=p_recv.at[s, p],
                 device_id=device(ahead[s], c), device_id_type=MESH)
-            pl.when((z > 0) | (ahead[s] > 0))(cp.start)
+            pl.when((ahead[s] > 0) | (z > 0) & (p < own - skip * (nz - 1 - z)) if skip else (ahead[s] > 0) | (z > 0))(cp.start)
             p_copies[s, p] = cp
         forward(nx - 1, p, prefix[x, p])
 
@@ -308,10 +334,10 @@
     ready = {}
     for n in range(own):
         ready[0, nx - 1, n] = n + lag
-        ready[1, nx - 1, n] = n + lag + 2
+        ready[1, nx - 1, n] = n + lag + LATE
     for n, (s, p) in enumerate(rest):
         ready[0, s, p] = n + own
-        ready[1, s, p] = n + own + 2
+        ready[1, s, p] = n + own + LATE
     slots = own + len(rest)
     waiting = sorted(ready, key=lambda one: (ready[one], one))
     todo = list(every)
@@ -319,15 +345,15 @@
     for slot in range(slots):
         if slot < own:
             fold(slot)
+        count = -(-len(todo) // max(own - slot, 1))
+        local(todo[:count])
+        todo = todo[count:]
         if lag <= slot < own + lag:
             spread(slot - lag)
         if slot >= own:
             s, p = rest[slot - own]
             pl.when((z > 0) | (x > 0))(p_copies[s, p].wait_recv)
             forward(s, p, pin[s * own + p])
-        count = -(-len(todo) // max(own - slot, 1))
-        local(todo[:count])
-        todo = todo[count:]
         now = [one for one in waiting if ready[one] <= slot and one not in todo]
         if len(now) >= BATCH:
             total = finish(now[:BATCH], total)
@@ -345,20 +371,28 @@
 
     sent(tsend, tt.at[c], s_send, s_recv.at[0, 0])
     if nx > 1:
-        sent(early, early, e_send, e_recv.at[0])
-        late = pl.ds(1, (nx - 1) * own - 1)
-        sent(xout.at[late], xout.at[late], t_send, t_recv.at[0, 0])
-
-        @pl.when((z > 0) | (x == 0))
+        @pl.when(tails_used)
         def _():
-            sent(pin, pin, p_send, p_recv.at[0, 0])
-
-    if nx > 2:
-        @pl.when((z == 0) & (x > 0))
-        def _():
-            most = pl.ds(0, (nx - 2) * own)
-            sent(pin.at[most], pin.at[most], p_send, p_recv.at[0, 0])
-
+            late = pl.ds(1, (nx - 1) * own - 1)
+            sent(early, early, e_send, e_recv.at[0])
+            sent(xout.at[late], xout.at[late], t_send, t_recv.at[0, 0])
+
+    def sent_prefixes(cond, count):
+        if count > 0:
+            @pl.when(cond)
+            def _():
+                part = pl.ds(0, count)
+                sent(pin.at[part], pin.at[part], p_send, p_recv.at[0, 0])
+
+    if skip:
+        sent_prefixes(x == 0, own)
+        for zz in range(1, nz):
+            sent_prefixes((x > 0) & (z == zz), own - skip * (nz - 1 - zz))
+        for cp, cond in skips:
+            pl.when(cond)(cp.wait_send)
+    else:
+        sent_prefixes((z > 0) | (x == 0), (nx - 1) * own)
+        sent_prefixes((z == 0) & (x > 0), (nx - 2) * own)
     sent(st.at[o], fin, f_send, f_recv.at[0, 0])
 
     @pl.when(z < nz - 1)
@@ -366,21 +400,18 @@
         sent(zout, zin, z_send, z_recv.at[0])
 
 
-def scale_kernel(parts, att_ref, scale_ref, gain_ref, out_hbm, buf, sems):
+def scale_kernel(parts, att_ref, scale_ref, gain_ref, out_hbm, buf, sem):
     rows, width = att_ref.shape
-    part = width // parts
-    scale = scale_ref[...]
-    copies = []
+    part = rows // parts
     for j in range(parts):
-        for i in range(part // DH):
-            at = j * part + i * DH
-            v = att_ref[:, at:at + DH].astype(F32)
-            buf[j, :, i * DH:(i + 1) * DH] = (v * scale * gain_ref[0:1, at:at + DH]).astype(BF16)
-        cp = pltpu.make_async_copy(buf.at[j], out_hbm.at[:, j * part:(j + 1) * part], sems.at[j])
-        cp.start()
-        copies.append(cp)
-    for cp in copies:
-        cp.wait()
+        at = pl.ds(j * part, part)
+        scale = scale_ref[at, :]
+        for i in range(width // DH):
+            col = pl.ds(i * DH, DH)
+            v = att_ref[at, col].astype(F32)
+            buf[at, col] = (v * scale * gain_ref[0:1, col]).astype(BF16)
+        pltpu.make_async_copy(buf.at[at], out_hbm.at[at], sem).start()
+    pltpu.make_async_copy(buf, out_hbm, sem).wait()
 
 
 def per_device(nz, nh, queries, keys_in, values, doc_lengths, rms_gain):
@@ -427,18 +458,18 @@
             dma(()), dma((own,)),
             dma(()), dma((far, own)),
             dma(()), dma((nx, own)),
-            dma(()), dma((2,)),
+            dma(()), dma((2,)), dma((max(1, SKIP * (nz - 2)) if nx == 2 else 1,)),
         ],
         compiler_params=pltpu.CompilerParams(collective_id=0, has_side_effects=True, vmem_limit_bytes=LIMIT1),
         name="scan_attention",
     )(pltpu.with_memory_space_constraint(doc_lengths, pltpu.HBM), queries, keys_in, values)
-    parts = 4
+    parts = 8
     return pl.pallas_call(
         functools.partial(scale_kernel, parts),
         out_shape=jax.ShapeDtypeStruct((rows, width), BF16),
         in_specs=[pl.BlockSpec(memory_space=pltpu.VMEM)] * 3,
         out_specs=pl.BlockSpec(memory_space=pl.ANY),
-        scratch_shapes=[pltpu.VMEM((parts, rows, width // parts), BF16), dma((parts,))],
+        scratch_shapes=[pltpu.VMEM((rows, width), BF16), dma(())],
         compiler_params=pltpu.CompilerParams(vmem_limit_bytes=LIMIT2),
         name="scale_rows",
     )(attended, scale, rms_gain.reshape(1, width))

time: 19.3 us -> 19.3 us (level)
  no operation moved by 1% of the time
where the time goes in v4:
time: 19.3 us; the launch traced here: 19.1 us
  Pallas kernels  19.1 us (99%)
    pallas_call x1, Pallas kernels, per_device(): pl.pallas_call(functools.partial(kernel, nz, nh, group), out_shape=(jax.S...  18.1 us
    pallas_call x1, Pallas kernels, per_device(): pl.pallas_call(functools.partial(scale_kernel, parts), out_shape=jax.Shap...  1 us

profile of v4, /device:TPU:9, one launch (start us, length us, event | category | flops | bytes accessed | tf_op | source)
XLA Modules:
  0.0 19.1 jit_solution(65332240688825291)
XLA Ops:
  0.0 0.0 copy-start
  0.0 18.1 %scan_attention.1 = (bf16[128,4096]{1,0:T(8,128)(2,1)S(1)}, f32[128,128]{1,0:T(8,128)S(1)}) custom-call(s32[5]{0:T(128)} %docs_hbm.1, bf16[128,4096]{1,0:T(8,128)(2,1)} %q_hbm.1, bf16[128,4096]{1,0:T(8,128)(2,1)} %k_hbm.1, bf16[128,4096]{1,0:T(8,128)(2,1)} %v_hbm.1), custom_call_target="tpu_custom_call" | custom-call | tf_op jit(solution)/shard_map/scan_attention/pallas_call | solution.py:431
  18.1 0.0 copy-done
  18.1 1.0 %scale_rows.1 = bf16[128,4096]{1,0:T(8,128)(2,1)} custom-call(bf16[128,4096]{1,0:T(8,128)(2,1)S(1)} %get-tuple-element.7.att_ref, f32[128,128]{1,0:T(8,128)S(1)} %get-tuple-element.8.scale_ref, f32[1,4096]{1,0:T(1,128)S(1)} %bitcast.1), custom_call_target="tpu_custom_call" | custom-call | tf_op jit(solution)/shard_map/scale_rows/pallas_call | solution.py:467
Async XLA Ops:
  0.0 18.1 %copy-start = (f32[4096]{0:T(1024)S(1)}, f32[4096]{0:T(1024)}, u32[]{:S(2)}) copy-start(f32[4096]{0:T(1024)} %param.9) | copy-start | bytes 49156

commit v5 on v4

--- a/solution.py
+++ b/solution.py
@@ -14,7 +14,6 @@
 F32 = jnp.float32
 BF16 = jnp.bfloat16
 BATCH = 4
-SKIP = 0
 LATE = 4
 
 
@@ -25,8 +24,8 @@
 
 
 def kernel(nz, nh, group, docs_hbm, q_hbm, k_hbm, v_hbm, out_ref, scale_ref,
-           ends_ref, doc_sem, qb, kb, vb, wq, maskb, joinb, keepb, tsend, tt, xout, tin, partial, zin, zout, prefix, pin, st, fin, early,
-           load_sem, s_send, s_recv, t_send, t_recv, z_send, z_recv, p_send, p_recv, f_send, f_recv, e_send, e_recv, d_send):
+           ends_ref, doc_sem, qb, kb, vb, wq, maskb, joinb, keepb, tsend, tt, xout, tin, partial, zin, zout, prefix, pin, st, fin, early, direct,
+           load_sem, s_send, s_recv, t_send, t_recv, z_send, z_recv, p_send, p_recv, f_send, f_recv, e_send, e_recv, d_send, d_recv):
     nx = nh // 2
     rows, width = q_hbm.shape
     heads = width // DH
@@ -37,7 +36,6 @@
     shard = nx * chunk
     longest = nz * shard // nh
     chained = longest > shard
-    skip = SKIP if nx == 2 and not chained else 0
     z = lax.axis_index("ctx")
     h = lax.axis_index("head")
     x = h // 2
@@ -78,15 +76,6 @@
     pl.semaphore_signal(barrier, inc=1, device_id=device(x, o), device_id_type=MESH)
     for s in range(nx - 1):
         pl.semaphore_signal(barrier, inc=1, device_id=device(ahead[s], c), device_id_type=MESH)
-
-    if skip:
-        @pl.when((x == 0) & (z > 0))
-        def _():
-            pl.semaphore_signal(barrier, inc=1, device_id=device(1, c, z - 1), device_id_type=MESH)
-
-        @pl.when((x > 0) & (z < nz - 1))
-        def _():
-            pl.semaphore_signal(barrier, inc=1, device_id=device(0, c, z + 1), device_id_type=MESH)
 
     across = [ahead[0], behind[0]][:min(nx - 1, 2)]
     for xx in across:
@@ -108,14 +97,13 @@
     q_copy = pltpu.make_async_copy(q_hbm, qb, load_sem.at[nx + 1])
     q_copy.start()
 
-    def activate(s, g):
-        for i in range(group):
-            for side in (1, 0):
-                at = cols(first_head(side, s, g) + i)
-                kb[:, at] = silu(kb[:, at])
+    def activate(i):
+        for side in (1, 0):
+            at = cols(first_head(side, 0, 0) + i)
+            kb[:, at] = silu(kb[:, at])
 
     loaded(0, group)
-    activate(0, 0)
+    activate(0)
     docs_copy.wait()
     ends = [ends_ref[0]]
     for d in range(1, docs):
@@ -137,15 +125,15 @@
     seg_r = seg_of(row_i + first)
     keepb[...] = jnp.where(seg_r == seg_of(first + rows - 1), 1.0, 0.0).astype(BF16)
 
-    def tails(s, g):
+    def tails(s, g, begin=0, end=None):
         if s == 0 and g == 1:
             loaded(1, own - group)
         elif s and g == 0:
             loaded(s + 1, own)
-        for i in range(group):
+        for i in range(begin, group if end is None else end):
             for side in (1, 0):
                 at = cols(first_head(side, s, g) + i)
-                kk = kb[:, at] if s == 0 and g == 0 else silu(kb[:, at])
+                kk = kb[:, at] if s == 0 and g == 0 and i == 0 else silu(kb[:, at])
                 kb[:, at] = kk
                 t = lax.dot_general(kk * keepb[...], vb[:, at], (((0,), (0,)), ((), ())), preferred_element_type=F32).astype(BF16)
                 if side:
@@ -182,8 +170,8 @@
             pl.when(tails_used)(cp.start)
             t_copies[s, p] = cp
 
-    tails(0, 0)
-    pl.semaphore_wait(barrier, nx + len(across) + jnp.where(z > 0, 2 - x if skip else 1, 0) + jnp.where(z < nz - 1, 1 + x if skip else 1, 0))
+    tails(0, 0, 0, 1)
+    pl.semaphore_wait(barrier, nx + len(across) + jnp.where(z > 0, 1, 0) + jnp.where(z < nz - 1, 1, 0))
     e_copies = []
     if nx > 1:
         for n, (src, cc) in enumerate(((tt.at[c, 0, 0], c), (tsend.at[0, 0], o))):
@@ -192,6 +180,7 @@
                 device_id=device(ahead[0], cc), device_id_type=MESH)
             pl.when(tails_used)(cp.start)
             e_copies.append(cp)
+    tails(0, 0, 1)
     pass_tails(0, 0)
     joinb[...] = jnp.where(seg_r == seg_of(first - 1), 1.0, 0.0).astype(BF16)
     col_i = lax.broadcasted_iota(jnp.int32, (8, rows), 1)
@@ -216,6 +205,16 @@
     for s, g in order[len(order) - delay:]:
         join_tails(s, g)
 
+    last = (nx - 2, own - 1) if nx > 1 else None
+    if nx > 1:
+        base_copy = pltpu.make_async_remote_copy(
+            src_ref=tt.at[0, 0, own - 1], dst_ref=direct.at[0], send_sem=d_send.at[0], recv_sem=d_recv.at[0],
+            device_id=device(x, 1), device_id_type=MESH)
+        pl.when(c == 0)(base_copy.start)
+        direct_copy = pltpu.make_async_remote_copy(
+            src_ref=prefix.at[ahead[nx - 2], own - 1], dst_ref=direct.at[1], send_sem=d_send.at[1], recv_sem=d_recv.at[1],
+            device_id=device(ahead[nx - 2], 1), device_id_type=MESH)
+
     q_copy.wait()
 
     def head_of(side, s, p):
@@ -237,6 +236,7 @@
     @pl.when((z == 0) & (x == 0))
     def _():
         pin[...] = jnp.zeros_like(pin)
+        direct[1] = jnp.zeros_like(direct[1])
 
     def z_copy(p):
         return pltpu.make_async_remote_copy(
@@ -274,15 +274,6 @@
         def _():
             z_copy(p).start()
 
-        if p >= own - skip * (nz - 2):
-            cp = pltpu.make_async_remote_copy(
-                src_ref=zout.at[p], dst_ref=pin.at[p], send_sem=d_send.at[own - 1 - p], recv_sem=p_recv.at[0, p],
-                device_id=device(0, c, z + 1), device_id_type=MESH)
-            cond = (x > 0) & (p >= own - skip * (nz - 2 - z))
-            pl.when(cond)(cp.start)
-            skips.append((cp, cond))
-
-    skips = []
     p_copies = {}
     f_copies = {}
 
@@ -291,9 +282,12 @@
         st[0, s, p] = state
         st[1, s, p] = into.astype(BF16)
         cp = pltpu.make_async_remote_copy(
-            src_ref=st.at[o, s, p], dst_ref=fin.at[s, p], send_sem=f_send, recv_sem=f_recv.at[s, p],
+            src_ref=st.at[o, s, p], dst_ref=fin.at[s * own + p], send_sem=f_send, recv_sem=f_recv.at[s, p],
             device_id=device(x, o), device_id_type=MESH)
-        cp.start()
+        if (s, p) == last:
+            pl.when(c > 0)(cp.start)
+        else:
+            cp.start()
         f_copies[s, p] = cp
 
     def spread(p):
@@ -306,21 +300,31 @@
             passed = passed * cont[xx]
             prefix[xx + 1, p] = (partial[p, xx] + carried * passed).astype(BF16)
         for s in range(nx - 1):
+            if (s, p) == last:
+                pl.when((c == 0) & ((z > 0) | (ahead[s] > 0)))(direct_copy.start)
             cp = pltpu.make_async_remote_copy(
                 src_ref=prefix.at[ahead[s], p], dst_ref=pin.at[s * own + p],
                 send_sem=p_send, recv_sem=p_recv.at[s, p],
                 device_id=device(ahead[s], c), device_id_type=MESH)
-            pl.when((ahead[s] > 0) | (z > 0) & (p < own - skip * (nz - 1 - z)) if skip else (ahead[s] > 0) | (z > 0))(cp.start)
+            pl.when((z > 0) | (ahead[s] > 0))(cp.start)
             p_copies[s, p] = cp
         forward(nx - 1, p, prefix[x, p])
 
     def finish(batch, total):
         for side, s, p in batch:
-            if side:
+            if side and (s, p) == last:
+                pl.when(c == 0)(f_copies[s, p].wait_recv)
+
+                @pl.when(c > 0)
+                def _():
+                    base_copy.wait_recv()
+                    pl.when((z > 0) | (x > 0))(direct_copy.wait_recv)
+                    fin[s * own + p] = (direct[0].astype(F32) + direct[1].astype(F32) * low).astype(BF16)
+            elif side:
                 f_copies[s, p].wait_recv()
         for side, s, p in batch:
             head = head_of(side, s, p)
-            state = fin[s, p] if side else st[c, s, p]
+            state = fin[s * own + p] if side else st[c, s, p]
             both = jnp.concatenate([vb[:, cols(head)], state], axis=0)
             att = jnp.dot(wq[head], both, preferred_element_type=F32).astype(BF16)
             out_ref[:, cols(head)] = att
@@ -384,16 +388,22 @@
                 part = pl.ds(0, count)
                 sent(pin.at[part], pin.at[part], p_send, p_recv.at[0, 0])
 
-    if skip:
-        sent_prefixes(x == 0, own)
-        for zz in range(1, nz):
-            sent_prefixes((x > 0) & (z == zz), own - skip * (nz - 1 - zz))
-        for cp, cond in skips:
-            pl.when(cond)(cp.wait_send)
-    else:
-        sent_prefixes((z > 0) | (x == 0), (nx - 1) * own)
-        sent_prefixes((z == 0) & (x > 0), (nx - 2) * own)
-    sent(st.at[o], fin, f_send, f_recv.at[0, 0])
+    sent_prefixes((z > 0) | (x == 0), (nx - 1) * own)
+    sent_prefixes((z == 0) & (x > 0), (nx - 2) * own)
+    def sent_states(cond, count):
+        @pl.when(cond)
+        def _():
+            part = pl.ds(0, count)
+            sent(fin.at[part], fin.at[part], f_send, f_recv.at[0, 0])
+
+    sent_states(c == 0, nx * own - (1 if nx > 1 else 0))
+    sent_states(c > 0, nx * own)
+    if nx > 1:
+        @pl.when(c == 0)
+        def _():
+            base_copy.wait_send()
+
+        pl.when((c == 0) & ((z > 0) | (ahead[nx - 2] > 0)))(direct_copy.wait_send)
 
     @pl.when(z < nz - 1)
     def _():
@@ -450,7 +460,8 @@
             vmem((nx, own, DH, DH), BF16),
             vmem((far * own, DH, DH), BF16),
             vmem((2, nx, own, DH, DH), BF16),
-            vmem((nx, own, DH, DH), BF16),
+            vmem((nx * own, DH, DH), BF16),
+            vmem((2, DH, DH), BF16),
             vmem((2, DH, DH), BF16),
             dma((nx + 2,)),
             dma(()), dma((nx, groups)),
@@ -458,7 +469,8 @@
             dma(()), dma((own,)),
             dma(()), dma((far, own)),
             dma(()), dma((nx, own)),
-            dma(()), dma((2,)), dma((max(1, SKIP * (nz - 2)) if nx == 2 else 1,)),
+            dma(()), dma((2,)),
+            dma((2,)), dma((2,)),
         ],
         compiler_params=pltpu.CompilerParams(collective_id=0, has_side_effects=True, vmem_limit_bytes=LIMIT1),
         name="scan_attention",

time: 19.3 us -> 19 us (0.984)
  Pallas kernels: 19.1 us -> 18.9 us
    pallas_call x1, Pallas kernels: 18.1 us -> 17.9 us  [per_device(): pl.pallas_call(functools.partial(kernel, nz, nh, group), out_shape=(jax.S...]
where the time goes in v5:
time: 19 us; the launch traced here: 18.9 us
  Pallas kernels  18.9 us (99%)
    pallas_call x1, Pallas kernels, per_device(): pl.pallas_call(functools.partial(kernel, nz, nh, group), out_shape=(jax.S...  17.9 us
    pallas_call x1, Pallas kernels, per_device(): pl.pallas_call(functools.partial(scale_kernel, parts), out_shape=jax.Shap...  1 us

profile of v5, /device:TPU:9, one launch (start us, length us, event | category | flops | bytes accessed | tf_op | source)
XLA Modules:
  0.0 18.9 jit_solution(5890259807965591504)
XLA Ops:
  0.0 0.0 copy-start
  0.0 17.9 %scan_attention.1 = (bf16[128,4096]{1,0:T(8,128)(2,1)S(1)}, f32[128,128]{1,0:T(8,128)S(1)}) custom-call(s32[5]{0:T(128)} %docs_hbm.1, bf16[128,4096]{1,0:T(8,128)(2,1)} %q_hbm.1, bf16[128,4096]{1,0:T(8,128)(2,1)} %k_hbm.1, bf16[128,4096]{1,0:T(8,128)(2,1)} %v_hbm.1), custom_call_target="tpu_custom_call" | custom-call | tf_op jit(solution)/shard_map/scan_attention/pallas_call | solution.py:441
  17.9 0.0 copy-done
  17.9 1.0 %scale_rows.1 = bf16[128,4096]{1,0:T(8,128)(2,1)} custom-call(bf16[128,4096]{1,0:T(8,128)(2,1)S(1)} %get-tuple-element.7.att_ref, f32[128,128]{1,0:T(8,128)S(1)} %get-tuple-element.8.scale_ref, f32[1,4096]{1,0:T(1,128)S(1)} %bitcast.1), custom_call_target="tpu_custom_call" | custom-call | tf_op jit(solution)/shard_map/scale_rows/pallas_call | solution.py:479
Async XLA Ops:
  0.0 17.9 %copy-start = (f32[4096]{0:T(1024)S(1)}, f32[4096]{0:T(1024)}, u32[]{:S(2)}) copy-start(f32[4096]{0:T(1024)} %param.9) | copy-start | bytes 49156

commit v6 on v5

--- a/solution.py
+++ b/solution.py
@@ -14,7 +14,7 @@
 F32 = jnp.float32
 BF16 = jnp.bfloat16
 BATCH = 4
-LATE = 4
+LATE = 3
 
 
 def silu(v):
@@ -24,8 +24,8 @@
 
 
 def kernel(nz, nh, group, docs_hbm, q_hbm, k_hbm, v_hbm, out_ref, scale_ref,
-           ends_ref, doc_sem, qb, kb, vb, wq, maskb, joinb, keepb, tsend, tt, xout, tin, partial, zin, zout, prefix, pin, st, fin, early, direct,
-           load_sem, s_send, s_recv, t_send, t_recv, z_send, z_recv, p_send, p_recv, f_send, f_recv, e_send, e_recv, d_send, d_recv):
+           ends_ref, doc_sem, qb, kb, vb, wq, maskb, joinb, keepb, tsend, tt, xout, tin, partial, zin, zout, prefix, pin, st, fin, early, direct, sums,
+           load_sem, s_send, s_recv, t_send, t_recv, z_send, z_recv, p_send, p_recv, f_recv, e_recv, d_recv):
     nx = nh // 2
     rows, width = q_hbm.shape
     heads = width // DH
@@ -142,9 +142,11 @@
                     tt[c, s, g * group + i] = t
 
     s_copies = {}
+    wide = 2 if groups % 2 == 0 else 1
 
     def pass_tails(s, g):
-        at = pl.ds(g * group, group)
+        count = wide if s else 1
+        at = pl.ds((g + 1 - count) * group, count * group)
         cp = pltpu.make_async_remote_copy(
             src_ref=tsend.at[s, at], dst_ref=tt.at[c, s, at], send_sem=s_send, recv_sem=s_recv.at[s, g],
             device_id=device(x, o), device_id_type=MESH)
@@ -154,7 +156,8 @@
     t_copies = {}
 
     def join_tails(s, g):
-        s_copies[s, g].wait_recv()
+        if s == 0 or g % wide == 0:
+            s_copies[s, g if s == 0 else g + wide - 1].wait_recv()
         for i in range(group):
             p = g * group + i
             if s == 0 and p == 0 and nx > 1:
@@ -176,7 +179,7 @@
     if nx > 1:
         for n, (src, cc) in enumerate(((tt.at[c, 0, 0], c), (tsend.at[0, 0], o))):
             cp = pltpu.make_async_remote_copy(
-                src_ref=src, dst_ref=early.at[c], send_sem=e_send, recv_sem=e_recv.at[n],
+                src_ref=src, dst_ref=early.at[c], send_sem=t_send, recv_sem=t_recv.at[0, 0] if n == 0 else e_recv,
                 device_id=device(ahead[0], cc), device_id_type=MESH)
             pl.when(tails_used)(cp.start)
             e_copies.append(cp)
@@ -199,7 +202,8 @@
     for n, (s, g) in enumerate(order):
         if n:
             tails(s, g)
-            pass_tails(s, g)
+            if s == 0 or g % wide == wide - 1:
+                pass_tails(s, g)
         if n >= delay:
             join_tails(*order[n - delay])
     for s, g in order[len(order) - delay:]:
@@ -208,11 +212,11 @@
     last = (nx - 2, own - 1) if nx > 1 else None
     if nx > 1:
         base_copy = pltpu.make_async_remote_copy(
-            src_ref=tt.at[0, 0, own - 1], dst_ref=direct.at[0], send_sem=d_send.at[0], recv_sem=d_recv.at[0],
+            src_ref=tt.at[0, 0, own - 1], dst_ref=direct.at[0], send_sem=s_send, recv_sem=d_recv.at[0],
             device_id=device(x, 1), device_id_type=MESH)
         pl.when(c == 0)(base_copy.start)
         direct_copy = pltpu.make_async_remote_copy(
-            src_ref=prefix.at[ahead[nx - 2], own - 1], dst_ref=direct.at[1], send_sem=d_send.at[1], recv_sem=d_recv.at[1],
+            src_ref=prefix.at[ahead[nx - 2], own - 1], dst_ref=direct.at[1], send_sem=p_send, recv_sem=d_recv.at[1],
             device_id=device(ahead[nx - 2], 1), device_id_type=MESH)
 
     q_copy.wait()
@@ -282,7 +286,7 @@
         st[0, s, p] = state
         st[1, s, p] = into.astype(BF16)
         cp = pltpu.make_async_remote_copy(
-            src_ref=st.at[o, s, p], dst_ref=fin.at[s * own + p], send_sem=f_send, recv_sem=f_recv.at[s, p],
+            src_ref=st.at[o, s, p], dst_ref=fin.at[s * own + p], send_sem=s_send, recv_sem=f_recv.at[s, p],
             device_id=device(x, o), device_id_type=MESH)
         if (s, p) == last:
             pl.when(c > 0)(cp.start)
@@ -359,12 +363,24 @@
             pl.when((z > 0) | (x > 0))(p_copies[s, p].wait_recv)
             forward(s, p, pin[s * own + p])
         now = [one for one in waiting if ready[one] <= slot and one not in todo]
-        if len(now) >= BATCH:
+        if len(now) >= (BATCH if slot < own else 2):
             total = finish(now[:BATCH], total)
             waiting = [one for one in waiting if one not in now[:BATCH]]
-    while waiting:
-        total = finish(waiting[:2], total)
-        waiting = waiting[2:]
+    sums[...] = total
+
+    @pl.when(c == 0)
+    def _():
+        sums[...] = finish(waiting, sums[...])
+
+    @pl.when(c > 0)
+    def _():
+        ends_with = [(1, *one) for one in rest[-1:] + rest[-2:-1]]
+        others = [one for one in waiting if one not in ends_with]
+        sums[...] = finish(others, sums[...])
+        for one in ends_with:
+            sums[...] = finish([one], sums[...])
+
+    total = sums[...]
     scale = lax.rsqrt(jnp.sum(total, axis=1, keepdims=True) / width + 1e-05)
     scale_ref[...] = jnp.broadcast_to(scale, (rows, DH))
 
@@ -373,37 +389,21 @@
             src_ref=src, dst_ref=dst, send_sem=sem, recv_sem=recv,
             device_id=device(x, o), device_id_type=MESH).wait_send()
 
-    sent(tsend, tt.at[c], s_send, s_recv.at[0, 0])
-    if nx > 1:
-        @pl.when(tails_used)
-        def _():
-            late = pl.ds(1, (nx - 1) * own - 1)
-            sent(early, early, e_send, e_recv.at[0])
-            sent(xout.at[late], xout.at[late], t_send, t_recv.at[0, 0])
-
-    def sent_prefixes(cond, count):
+    def sent_if(cond, count, sem):
         if count > 0:
             @pl.when(cond)
             def _():
                 part = pl.ds(0, count)
-                sent(pin.at[part], pin.at[part], p_send, p_recv.at[0, 0])
-
-    sent_prefixes((z > 0) | (x == 0), (nx - 1) * own)
-    sent_prefixes((z == 0) & (x > 0), (nx - 2) * own)
-    def sent_states(cond, count):
-        @pl.when(cond)
-        def _():
-            part = pl.ds(0, count)
-            sent(fin.at[part], fin.at[part], f_send, f_recv.at[0, 0])
-
-    sent_states(c == 0, nx * own - (1 if nx > 1 else 0))
-    sent_states(c > 0, nx * own)
+                sent(fin.at[part], fin.at[part], sem, s_recv.at[0, 0])
+
+    sent(tt, tt, s_send, s_recv.at[0, 0])
     if nx > 1:
-        @pl.when(c == 0)
-        def _():
-            base_copy.wait_send()
-
-        pl.when((c == 0) & ((z > 0) | (ahead[nx - 2] > 0)))(direct_copy.wait_send)
+        sent_if(tails_used, (nx - 1) * own + 1, t_send)
+        whole = (z > 0) | (x == 0)
+        straight = (c == 0) & ((z > 0) | (ahead[nx - 2] > 0))
+        for cond, count in ((whole, (nx - 1) * own), (~whole, (nx - 2) * own)):
+            sent_if(cond & straight, count + 1, p_send)
+            sent_if(cond & ~straight, count, p_send)
 
     @pl.when(z < nz - 1)
     def _():
@@ -463,14 +463,15 @@
             vmem((nx * own, DH, DH), BF16),
             vmem((2, DH, DH), BF16),
             vmem((2, DH, DH), BF16),
+            vmem((rows, DH), F32),
             dma((nx + 2,)),
             dma(()), dma((nx, groups)),
             dma(()), dma((far, own)),
             dma(()), dma((own,)),
             dma(()), dma((far, own)),
-            dma(()), dma((nx, own)),
-            dma(()), dma((2,)),
-            dma((2,)), dma((2,)),
+            dma((nx, own)),
+            dma(()),
+            dma((2,)),
         ],
         compiler_params=pltpu.CompilerParams(collective_id=0, has_side_effects=True, vmem_limit_bytes=LIMIT1),
         name="scan_attention",

time: 19 us -> 19 us (level)
  no operation moved by 1% of the time
where the time goes in v6:
time: 19 us; the launch traced here: 18.8 us
  Pallas kernels  18.8 us (99%)
    pallas_call x1, Pallas kernels, per_device(): pl.pallas_call(functools.partial(kernel, nz, nh, group), out_shape=(jax.S...  17.8 us
    pallas_call x1, Pallas kernels, per_device(): pl.pallas_call(functools.partial(scale_kernel, parts), out_shape=jax.Shap...  1 us

profile of v6, /device:TPU:9, one launch (start us, length us, event | category | flops | bytes accessed | tf_op | source)
XLA Modules:
  0.0 18.8 jit_solution(3844461540756072612)
XLA Ops:
  0.0 0.0 copy-start
  0.0 17.8 %scan_attention.1 = (bf16[128,4096]{1,0:T(8,128)(2,1)S(1)}, f32[128,128]{1,0:T(8,128)S(1)}) custom-call(s32[5]{0:T(128)} %docs_hbm.1, bf16[128,4096]{1,0:T(8,128)(2,1)} %q_hbm.1, bf16[128,4096]{1,0:T(8,128)(2,1)} %k_hbm.1, bf16[128,4096]{1,0:T(8,128)(2,1)} %v_hbm.1), custom_call_target="tpu_custom_call" | custom-call | tf_op jit(solution)/shard_map/scan_attention/pallas_call | solution.py:441
  17.8 0.0 copy-done
  17.8 1.0 %scale_rows.1 = bf16[128,4096]{1,0:T(8,128)(2,1)} custom-call(bf16[128,4096]{1,0:T(8,128)(2,1)S(1)} %get-tuple-element.7.att_ref, f32[128,128]{1,0:T(8,128)S(1)} %get-tuple-element.8.scale_ref, f32[1,4096]{1,0:T(1,128)S(1)} %bitcast.1), custom_call_target="tpu_custom_call" | custom-call | tf_op jit(solution)/shard_map/scale_rows/pallas_call | solution.py:480
Async XLA Ops:
  0.0 17.8 %copy-start = (f32[4096]{0:T(1024)S(1)}, f32[4096]{0:T(1024)}, u32[]{:S(2)}) copy-start(f32[4096]{0:T(1024)} %param.9) | copy-start | bytes 49156

commit v7 on v6

--- a/solution.py
+++ b/solution.py
@@ -148,7 +148,7 @@
         count = wide if s else 1
         at = pl.ds((g + 1 - count) * group, count * group)
         cp = pltpu.make_async_remote_copy(
-            src_ref=tsend.at[s, at], dst_ref=tt.at[c, s, at], send_sem=s_send, recv_sem=s_recv.at[s, g],
+            src_ref=tsend.at[s, at], dst_ref=tt.at[c, s, at], send_sem=s_send, recv_sem=s_recv.at[g if s == 0 else groups + (s - 1) * (groups // wide) + g // wide],
             device_id=device(x, o), device_id_type=MESH)
         cp.start()
         s_copies[s, g] = cp
@@ -198,7 +198,7 @@
     cont = [spans(shard_start + xx * chunk, chunk) for xx in range(nx)]
 
     order = [(s, g) for s in range(nx) for g in range(groups)]
-    delay = min(3, len(order) - 1)
+    delay = min(4, len(order) - 1)
     for n, (s, g) in enumerate(order):
         if n:
             tails(s, g)
@@ -394,9 +394,9 @@
             @pl.when(cond)
             def _():
                 part = pl.ds(0, count)
-                sent(fin.at[part], fin.at[part], sem, s_recv.at[0, 0])
-
-    sent(tt, tt, s_send, s_recv.at[0, 0])
+                sent(fin.at[part], fin.at[part], sem, s_recv.at[0])
+
+    sent(tt, tt, s_send, s_recv.at[0])
     if nx > 1:
         sent_if(tails_used, (nx - 1) * own + 1, t_send)
         whole = (z > 0) | (x == 0)
@@ -465,7 +465,7 @@
             vmem((2, DH, DH), BF16),
             vmem((rows, DH), F32),
             dma((nx + 2,)),
-            dma(()), dma((nx, groups)),
+            dma(()), dma((groups + (nx - 1) * (groups // (2 if groups % 2 == 0 else 1)),)),
             dma(()), dma((far, own)),
             dma(()), dma((own,)),
             dma(()), dma((far, own)),

time: 19 us -> 19 us (level)
  no operation moved by 1% of the time
where the time goes in v7:
time: 19 us; the launch traced here: 18.8 us
  Pallas kernels  18.8 us (99%)
    pallas_call x1, Pallas kernels, per_device(): pl.pallas_call(functools.partial(kernel, nz, nh, group), out_shape=(jax.S...  17.8 us
    pallas_call x1, Pallas kernels, per_device(): pl.pallas_call(functools.partial(scale_kernel, parts), out_shape=jax.Shap...  1 us

profile of v7, /device:TPU:9, one launch (start us, length us, event | category | flops | bytes accessed | tf_op | source)
XLA Modules:
  0.0 18.8 jit_solution(14422781136344444574)
XLA Ops:
  0.0 0.0 copy-start
  0.0 17.8 %scan_attention.1 = (bf16[128,4096]{1,0:T(8,128)(2,1)S(1)}, f32[128,128]{1,0:T(8,128)S(1)}) custom-call(s32[5]{0:T(128)} %docs_hbm.1, bf16[128,4096]{1,0:T(8,128)(2,1)} %q_hbm.1, bf16[128,4096]{1,0:T(8,128)(2,1)} %k_hbm.1, bf16[128,4096]{1,0:T(8,128)(2,1)} %v_hbm.1), custom_call_target="tpu_custom_call" | custom-call | tf_op jit(solution)/shard_map/scan_attention/pallas_call | solution.py:441
  17.8 0.0 copy-done
  17.8 1.0 %scale_rows.1 = bf16[128,4096]{1,0:T(8,128)(2,1)} custom-call(bf16[128,4096]{1,0:T(8,128)(2,1)S(1)} %get-tuple-element.7.att_ref, f32[128,128]{1,0:T(8,128)S(1)} %get-tuple-element.8.scale_ref, f32[1,4096]{1,0:T(1,128)S(1)} %bitcast.1), custom_call_target="tpu_custom_call" | custom-call | tf_op jit(solution)/shard_map/scale_rows/pallas_call | solution.py:480
Async XLA Ops:
  0.0 17.8 %copy-start = (f32[4096]{0:T(1024)S(1)}, f32[4096]{0:T(1024)}, u32[]{:S(2)}) copy-start(f32[4096]{0:T(1024)} %param.9) | copy-start | bytes 49156

commit v8 on v7

--- a/solution.py
+++ b/solution.py
@@ -142,7 +142,7 @@
                     tt[c, s, g * group + i] = t
 
     s_copies = {}
-    wide = 2 if groups % 2 == 0 else 1
+    wide = 4 if groups % 4 == 0 else 1
 
     def pass_tails(s, g):
         count = wide if s else 1
@@ -198,7 +198,7 @@
     cont = [spans(shard_start + xx * chunk, chunk) for xx in range(nx)]
 
     order = [(s, g) for s in range(nx) for g in range(groups)]
-    delay = min(4, len(order) - 1)
+    delay = min(3, len(order) - 1)
     for n, (s, g) in enumerate(order):
         if n:
             tails(s, g)
@@ -465,7 +465,7 @@
             vmem((2, DH, DH), BF16),
             vmem((rows, DH), F32),
             dma((nx + 2,)),
-            dma(()), dma((groups + (nx - 1) * (groups // (2 if groups % 2 == 0 else 1)),)),
+            dma(()), dma((groups + (nx - 1) * (groups // (4 if groups % 4 == 0 else 1)),)),
             dma(()), dma((far, own)),
             dma(()), dma((own,)),
             dma(()), dma((far, own)),

time: 19 us -> 19 us (level)
  no operation moved by 1% of the time
where the time goes in v8:
time: 19 us; the launch traced here: 18.8 us
  Pallas kernels  18.8 us (99%)
    pallas_call x1, Pallas kernels, per_device(): pl.pallas_call(functools.partial(kernel, nz, nh, group), out_shape=(jax.S...  17.8 us
    pallas_call x1, Pallas kernels, per_device(): pl.pallas_call(functools.partial(scale_kernel, parts), out_shape=jax.Shap...  1 us

profile of v8, /device:TPU:9, one launch (start us, length us, event | category | flops | bytes accessed | tf_op | source)
XLA Modules:
  0.0 18.8 jit_solution(12981259403645145587)
XLA Ops:
  0.0 0.0 copy-start
  0.0 17.8 %scan_attention.1 = (bf16[128,4096]{1,0:T(8,128)(2,1)S(1)}, f32[128,128]{1,0:T(8,128)S(1)}) custom-call(s32[5]{0:T(128)} %docs_hbm.1, bf16[128,4096]{1,0:T(8,128)(2,1)} %q_hbm.1, bf16[128,4096]{1,0:T(8,128)(2,1)} %k_hbm.1, bf16[128,4096]{1,0:T(8,128)(2,1)} %v_hbm.1), custom_call_target="tpu_custom_call" | custom-call | tf_op jit(solution)/shard_map/scan_attention/pallas_call | solution.py:441
  17.8 0.0 copy-done
  17.8 1.0 %scale_rows.1 = bf16[128,4096]{1,0:T(8,128)(2,1)} custom-call(bf16[128,4096]{1,0:T(8,128)(2,1)S(1)} %get-tuple-element.7.att_ref, f32[128,128]{1,0:T(8,128)S(1)} %get-tuple-element.8.scale_ref, f32[1,4096]{1,0:T(1,128)S(1)} %bitcast.1), custom_call_target="tpu_custom_call" | custom-call | tf_op jit(solution)/shard_map/scale_rows/pallas_call | solution.py:480
Async XLA Ops:
  0.0 17.8 %copy-start = (f32[4096]{0:T(1024)S(1)}, f32[4096]{0:T(1024)}, u32[]{:S(2)}) copy-start(f32[4096]{0:T(1024)} %param.9) | copy-start | bytes 49156
